TPU v7x, 32 devices: a whole 2x2x4 slice. The times are simulated.
32 devices in a mesh: seq: 16 (over z, x, core), hx: 2 (over y).
Axes of the slice: x: 2, y: 2, z: 4, core: 2. Of those that a mesh axis runs over, the one named last changes fastest.
Arguments:
- stream: float32 [16, 2048, 768], P('seq', 'hx'), may hold values from -6 to 6
- cotangent: float32 [16, 2048, 768], P('seq', 'hx'), may hold values from -6 to 6
- norm_gain: bfloat16 [768], P('seq'), may hold values from 0.5 to 1.5
- in_main: bfloat16 [768, 3328], P('seq'), may hold values from -0.21875 to 0.21875
- in_dt: bfloat16 [768, 24], P('seq'), may hold values from -0.21875 to 0.21875
- conv_weight: bfloat16 [4, 1792], P(None, 'seq'), may hold values from -3 to 3
- conv_bias: bfloat16 [1792], P('seq'), may hold values from -3 to 3
- dt_bias: float32 [24], replicated, may hold values from -6.9 to -2.25
- a_log: float32 [24], replicated, may hold values from 0 to 2.77
- skip_gain: float32 [24], replicated, may hold values from 0.5 to 2
- gated_gain: bfloat16 [1536], P('seq'), may hold values from 0.5 to 1.5
- out_weight: bfloat16 [1536, 768], P('seq'), may hold values from -0.15625 to 0.15625
Outputs:
- output: float32 [16, 2048, 768], P('seq', 'hx')
- grad_stream: float32 [16, 2048, 768], P('seq', 'hx')
- grad_norm_gain: float32 [768], P('seq')
- grad_in_main: float32 [768, 3328], P('seq')
- grad_in_dt: float32 [768, 24], P('seq')
- grad_conv_weight: float32 [4, 1792], P(None, 'seq')
- grad_conv_bias: float32 [1792], P('seq')
- grad_dt_bias: float32 [24], replicated
- grad_a_log: float32 [24], replicated
- grad_skip_gain: float32 [24], replicated
- grad_gated_gain: float32 [1536], P('seq')
- grad_out_weight: float32 [1536, 768], P('seq')
All inputs are finite; a program needn't handle non-finite values.
Results may differ from a plain program's by a relative error of at most 0.012.
Values may be sent and summed in bfloat16 or wider, within the bound.
No kernel may reach another device: no remote copies, remote signals or barrier semaphores. Data moves between devices by JAX's collectives and lax.ppermute only.
A program may use at most 192 MiB of HBM per device.

v0:
```python
import functools

import jax
import jax.numpy as jnp
from jax import lax
from jax.experimental import pallas as pl
from jax.experimental.pallas import tpu as pltpu
from jax.sharding import PartitionSpec as P

STATE = 128
CONV = 4
EPSILON = 1e-05
Q = 128
LANES = 128
GROUP = 256
WIDE = 2 * Q
HALO = 16
BF = jnp.bfloat16
F32 = jnp.float32
EXACT = lax.Precision.HIGHEST


def dot(a, b, precision=None):
    return lax.dot_general(
        a, b, (((1,), (0,)), ((), ())), precision=precision, preferred_element_type=F32
    )


def dot_nt(a, b):
    return lax.dot_general(a, b, (((1,), (1,)), ((), ())), preferred_element_type=F32)


def dot_tn(a, b):
    return lax.dot_general(a, b, (((0,), (0,)), ((), ())), preferred_element_type=F32)


def two_terms(v):
    hi = v.astype(BF)
    lo = (v - hi.astype(F32)).astype(BF)
    return jnp.concatenate([hi, lo], axis=1)


def softplus(v):
    return jnp.maximum(v, 0.0) + jnp.log1p(jnp.exp(-jnp.abs(v)))


def sigmoid(v):
    return 1.0 / (1.0 + jnp.exp(-v))


def three_terms(v):
    hi = v.astype(BF).astype(F32)
    mid = (v - hi).astype(BF).astype(F32)
    return hi, mid, (v - hi - mid).astype(BF).astype(F32)


def gap_left(cum, sign):
    hi, mid, lo = three_terms(sign * cum)
    lane = lax.broadcasted_iota(jnp.int32, cum.shape, 1)
    ones = jnp.where((lane >= 96) & (lane < 99), 1.0, 0.0)
    return (hi + pltpu.roll(mid, 32, 1) + pltpu.roll(lo, 64, 1) + ones).astype(BF)


def gap_right(cum_t, sign, heads, ref):
    hi, mid, lo = three_terms(sign * cum_t)
    zero = jnp.zeros((13, Q), F32)
    for h in range(heads):
        row = slice(h, h + 1)
        block = jnp.concatenate([hi[row], mid[row], lo[row], zero], axis=0)
        ref[96:112, Q * h : Q * (h + 1)] = block.astype(BF)


def root_of(v):
    return lax.rsqrt(jnp.mean(v * v, axis=-1, keepdims=True) + EPSILON)


def tri(rows, cols, keep):
    r = lax.broadcasted_iota(jnp.int32, (rows, cols), 0)
    c = lax.broadcasted_iota(jnp.int32, (rows, cols), 1)
    return keep(r, c)


def half_blocks(v, width):
    lane = lax.broadcasted_iota(jnp.int32, v.shape, 1)
    zero = jnp.zeros_like(v)
    return jnp.concatenate([jnp.where(lane < width, v, zero), jnp.where(lane >= width, v, zero)], axis=0)


def project_kernel(
    n,
    halo_ref,
    s_ref,
    wa_ref,
    wb_ref,
    hp_ref,
    ee_ref,
    shift_ref,
    nrm_ref,
    cin_ref,
    xc_ref,
    slope_ref,
    dtv_ref,
    cum_ref,
    base_ref,
    sloc_ref,
    fin_ref,
    tot_ref,
    small_ref,
    full,
    state,
    base,
):
    i = pl.program_id(0)
    cd = cin_ref.shape[1]
    di = fin_ref.shape[1]
    d, ca = wa_ref.shape
    rows = d // n

    def columns(lo, hi):
        if hi <= ca:
            return wa_ref[:, lo:hi]
        return wb_ref[:, lo - ca : hi - ca]

    @pl.when(i == 0)
    def _():
        small_ref[...] = jnp.zeros_like(small_ref)
        for k in range(n):
            piece = wb_ref[rows * k : rows * k + 8, cd + LANES - ca :].astype(F32)
            for row, size in ((0, d // n), (6, di // n)):
                small_ref[row : row + 1, size * k : size * (k + 1)] = piece[row : row + 1, :size]
            size = cd // n
            small_ref[1:6, size * k : size * (k + 1)] = piece[1:6, :size]
        h = halo_ref[...]
        nh = (h * root_of(h) * small_ref[0:1, :d]).astype(BF)
        nrm_ref[...] = jnp.zeros_like(nrm_ref)
        nrm_ref[WIDE - HALO :, :] = nh
        cin_ref[...] = jnp.zeros_like(cin_ref)
        ph = jnp.concatenate([dot(nh, columns(0, ca)), dot(nh, columns(ca, cd))], axis=1).astype(BF)
        cin_ref[WIDE - HALO :, :] = ph
        full[0:HALO, :] = ph
        state[...] = jnp.zeros_like(state)
        base[...] = jnp.zeros_like(base)

    @pl.when(i > 0)
    def _():
        s = s_ref[...]
        nrm = (s * root_of(s) * small_ref[0:1, :d]).astype(BF)
        nrm_ref[...] = nrm
        dtv = dot(nrm, columns(cd, cd + LANES)).astype(BF).astype(F32) + hp_ref[0:1, :]
        dtv_ref[...] = dtv
        step = softplus(dtv)
        lower = tri(Q, Q, lambda r, c: r >= c).astype(F32)
        weights, ends = [], []
        for p in range(WIDE // Q):
            part = slice(Q * p, Q * (p + 1))
            cum = dot(lower, hp_ref[1:2, :] * step[part], EXACT)
            cum_ref[part, :] = cum
            last = cum[Q - 1 : Q, :]
            base_ref[8 * p : 8 * (p + 1), :] = base[...]
            base[...] = base[...] + last
            weights.append(jnp.exp(last - cum) * step[part])
            ends.append(two_terms(jnp.broadcast_to(jnp.exp(last), (8, LANES))))
        weight = two_terms(jnp.concatenate(weights, axis=0))
        ends = jnp.concatenate(ends, axis=0)

        def conv(lo, hi):
            cin = dot(nrm, columns(lo, hi)).astype(BF)
            cin_ref[:, lo:hi] = cin
            full[HALO:, lo:hi] = cin
            earlier = [dot(shift_ref[...], full[Q * p : Q * (p + 1) + HALO, lo:hi]) for p in range(WIDE // Q)]
            summed = small_ref[5:6, lo:hi] + small_ref[4:5, lo:hi] * cin.astype(F32)
            for k in range(CONV - 1):
                rows_k = jnp.concatenate([e[Q * k : Q * (k + 1)] for e in earlier], axis=0)
                summed = summed + small_ref[k + 1 : k + 2, lo:hi] * rows_k
            full[0:HALO, lo:hi] = full[WIDE:, lo:hi]
            sig = sigmoid(summed)
            xc = summed * sig
            slope_ref[:, lo:hi] = (sig + xc * (1.0 - sig)).astype(BF)
            xcb = xc.astype(BF)
            xc_ref[:, lo:hi] = xcb
            return xc, xcb

        _, bc = conv(di, cd)
        bm = bc[:, :STATE]
        for lo in range(0, di, GROUP):
            cols = slice(lo, lo + GROUP)
            xc, _ = conv(lo, lo + GROUP)
            u = (dot(weight, ee_ref[:, cols]) * xc).astype(BF)
            fade = dot(ends, ee_ref[:, cols])
            now = state[:, cols]
            for p in range(WIDE // Q):
                part = slice(Q * p, Q * (p + 1))
                sloc_ref[p, :, cols] = now.astype(BF)
                now = now * fade[8 * p : 8 * p + 1] + dot_tn(bm[part], u[part])
            state[:, cols] = now

    @pl.when(i == pl.num_programs(0) - 1)
    def _():
        fin_ref[...] = state[...].astype(BF)
        tot_ref[...] = base[...]


def intra_kernel(width, xc_ref, dtv_ref, cum_ref, skip_ref, ee_ref, pick_ref, yi_ref, right):
    di = yi_ref.shape[1]

    @pl.when(pl.program_id(0) == 0)
    def _():
        right[...] = pick_ref[...]

    bm, cm = xc_ref[:, di : di + STATE], xc_ref[:, di + STATE :]
    cum = cum_ref[...]
    left = gap_left(cum, 1.0)
    gap_right(cum.T, -1.0, di // width, right)
    mix = jnp.where(tri(Q, Q, lambda r, c: r >= c), dot_nt(cm, bm), 0.0)
    step = two_terms(softplus(dtv_ref[...]))
    each = GROUP // width
    for lo in range(0, di, GROUP):
        cols = slice(lo, lo + GROUP)
        x = xc_ref[:, cols].astype(F32)
        ub = (dot(step, ee_ref[:, cols]) * x).astype(BF)
        first = lo // width
        gap = dot(left, right[:, Q * first : Q * (first + each)])
        parts = []
        for q in range(0, each, 2):
            two = [
                (jnp.exp(jnp.minimum(gap[:, Q * h : Q * (h + 1)], 0.0)) * mix).astype(BF) for h in (q, q + 1)
            ]
            pair = slice(q * width, (q + 2) * width)
            parts.append(dot(jnp.concatenate(two, axis=1), half_blocks(ub[:, pair], width)))
        yi_ref[:, cols] = (jnp.concatenate(parts, axis=1) + skip_ref[:, cols] * x).astype(BF)


def gate_kernel(
    n,
    yi_ref,
    nrm_ref,
    c_ref,
    cum_ref,
    base_ref,
    sloc_ref,
    hin_ref,
    s_ref,
    cot_ref,
    wzo_ref,
    small_ref,
    ee_ref,
    out_ref,
    mixed_ref,
    dsc_ref,
    dz_ref,
    start_ref,
    gst_ref,
    gst,
    wo,
    scan_s,
    z_s,
    weighted_s,
):
    i = pl.program_id(0)
    di = yi_ref.shape[1]
    d = s_ref.shape[1]

    @pl.when(i == 0)
    def _():
        gst[...] = jnp.zeros_like(gst)
        rows, per = d // n, di // d
        for k in range(n):
            for a in range(per):
                at = (per * k + a) * rows
                wo[at : at + rows, :] = wzo_ref[rows * k : rows * (k + 1), di + d * a : di + d * (a + 1)]

    halves = WIDE // Q
    nrm = nrm_ref[...]
    cm = c_ref[...]
    cotb = cot_ref[...].astype(BF)
    cum = cum_ref[...]
    bases = [base_ref[8 * p : 8 * p + 1, :] for p in range(halves)]
    ex_2 = two_terms(jnp.exp(cum))
    grow_2 = two_terms(jnp.concatenate([jnp.exp(cum[Q * p : Q * (p + 1)] + bases[p]) for p in range(halves)], axis=0))
    base_2 = two_terms(jnp.concatenate([jnp.broadcast_to(jnp.exp(b), (8, LANES)) for b in bases], axis=0))
    square = jnp.zeros((WIDE, LANES), F32)
    along = jnp.zeros((WIDE, LANES), F32)
    for lo in range(0, di, GROUP):
        cols = slice(lo, lo + GROUP)
        ee = ee_ref[:, cols]
        fade = dot(base_2, ee)
        inter = []
        for p in range(halves):
            start = (
                sloc_ref[p, :, cols].astype(F32) + fade[8 * p : 8 * p + 1] * hin_ref[:, cols].astype(F32)
            ).astype(BF)
            start_ref[p, :, cols] = start
            inter.append(dot(cm[Q * p : Q * (p + 1)], start))
        scb = (yi_ref[:, cols].astype(F32) + dot(ex_2, ee) * jnp.concatenate(inter, axis=0)).astype(BF)
        scan_s[:, cols] = scb
        z = dot(nrm, wzo_ref[:, cols])
        z_s[:, cols] = z
        gated = scb.astype(F32) * (z * sigmoid(z))
        weighted = small_ref[6:7, cols] * dot_nt(cotb, wo[cols, :])
        weighted_s[:, cols] = weighted
        for q in range(0, GROUP, LANES):
            g = gated[:, q : q + LANES]
            square = square + g * g
            along = along + g * weighted[:, q : q + LANES]
    inv = lax.rsqrt(jnp.sum(square, axis=-1, keepdims=True) / di + EPSILON)
    proj = inv * inv * (jnp.sum(along, axis=-1, keepdims=True) / di)
    for lo in range(0, di, GROUP):
        cols = slice(lo, lo + GROUP)
        scanned = scan_s[:, cols].astype(F32)
        z = z_s[:, cols]
        sig = sigmoid(z)
        silu = z * sig
        gated = scanned * silu
        mixed_ref[:, cols] = (gated * inv * small_ref[6:7, cols]).astype(BF)
        d_gated = inv * (weighted_s[:, cols] - gated * proj)
        dsc = (d_gated * silu).astype(BF)
        dsc_ref[:, cols] = dsc
        dz_ref[:, cols] = (d_gated * scanned * (sig + silu * (1.0 - sig))).astype(BF)
        grown = (dot(grow_2, ee_ref[:, cols]) * dsc.astype(F32)).astype(BF)
        gst[:, cols] = gst[:, cols] + dot_tn(cm, grown)
    out_ref[...] = s_ref[...] + dot(mixed_ref[...], wo[...])

    @pl.when(i == pl.num_programs(0) - 1)
    def _():
        gst_ref[...] = gst[...].astype(BF)


def scan_back_kernel(
    width,
    xc_ref,
    slope_ref,
    dtv_ref,
    cum_ref,
    start_ref,
    gin_ref,
    dsc_ref,
    cin_ref,
    prev_ref,
    small_ref,
    hp_ref,
    skip_ref,
    ee_ref,
    er_ref,
    hot_ref,
    pick_ref,
    shift_ref,
    d_ref,
    gconv_ref,
    ghead_ref,
    full_d,
    ds_state,
    kcol,
    right,
):
    i = pl.program_id(0)
    n = pl.num_programs(0) - 1
    di = dsc_ref.shape[1]
    cd = cin_ref.shape[1]

    def tap(k, cols=slice(None)):
        return small_ref[k + 1 : k + 2, cols]

    @pl.when(i == 0)
    def _():
        ds_state[...] = gin_ref[...].astype(F32)
        full_d[...] = jnp.zeros_like(full_d)
        kcol[...] = jnp.zeros_like(kcol)
        right[...] = pick_ref[...]
        gconv_ref[...] = jnp.zeros_like(gconv_ref)
        ghead_ref[...] = jnp.zeros_like(ghead_ref)

    @pl.when(i < n)
    def _():
        bm, cm = xc_ref[:, di : di + STATE], xc_ref[:, di + STATE :]
        dtv = dtv_ref[...]
        step = softplus(dtv)
        nega = hp_ref[1:2, :]
        cum = cum_ref[...]
        left = gap_left(cum, -1.0)
        gap_right(cum.T, 1.0, di // width, right)
        last = cum[Q - 1 : Q, :]
        causal = tri(Q, Q, lambda r, c: c >= r)
        mix_t = jnp.where(causal, dot_nt(bm, cm), 0.0)
        step_2 = two_terms(step)
        tail_2 = two_terms(jnp.exp(last - cum))
        ex_2 = two_terms(jnp.exp(cum))
        at_end = jnp.exp(last)
        end_2 = two_terms(jnp.broadcast_to(at_end, (8, LANES)))
        d_mix = jnp.zeros((Q, Q), F32)
        krow = jnp.zeros((Q, LANES), F32)
        d_b, d_c = jnp.zeros((Q, STATE), F32), jnp.zeros((Q, STATE), F32)
        sums = jnp.zeros((3 * Q, LANES), F32)
        row_sums = jnp.zeros((16, LANES), F32)

        def conv_back(cols, d_sum):
            full_d[0:Q, cols] = d_sum.astype(BF)
            laters = dot(shift_ref[...], full_d[:, cols])
            cin = cin_ref[:, cols].astype(F32)
            d_cin = tap(CONV - 1, cols) * d_sum
            gconv_ref[CONV - 1 : CONV, cols] += jnp.sum(d_sum * cin, axis=0, keepdims=True)
            gconv_ref[CONV : CONV + 1, cols] += jnp.sum(d_sum, axis=0, keepdims=True)
            for k in range(CONV - 1):
                later = laters[Q * k : Q * (k + 1)]
                d_cin = d_cin + tap(k, cols) * later
                gconv_ref[k : k + 1, cols] += jnp.sum(later * cin, axis=0, keepdims=True)
            d_ref[:, cols] = d_cin.astype(BF)
            full_d[Q:, cols] = full_d[0:HALO, cols]

        for lo in range(0, di, GROUP):
            cols = slice(lo, lo + GROUP)
            ee = ee_ref[:, cols]
            x = xc_ref[:, cols].astype(F32)
            dyb = dsc_ref[:, cols]
            dy = dyb.astype(F32)
            step_e = dot(step_2, ee)
            u = step_e * x
            ub = u.astype(BF)
            parts = []
            gap = dot(left, right[:, Q * (lo // width) : Q * ((lo + GROUP) // width)])
            for q in range(0, GROUP, 2 * width):
                pair = slice(q, q + 2 * width)
                dy_blocks = half_blocks(dyb[:, pair], width)
                d_m = dot_nt(ub[:, pair], dy_blocks)
                ms, ks = [], []
                first = (lo + q) // width
                for j in range(2):
                    h = first + j
                    at = Q * (h - lo // width)
                    fall = jnp.exp(jnp.minimum(gap[:, at : at + Q], 0.0))
                    m = mix_t * fall
                    d_one = d_m[:, Q * j : Q * (j + 1)]
                    d_mix = d_mix + d_one * fall
                    kb = (d_one * m).astype(BF)
                    kcol[h : h + 1, :] = jnp.sum(kb.astype(F32), axis=0, keepdims=True)
                    ms.append(m.astype(BF))
                    ks.append(kb)
                parts.append(dot(jnp.concatenate(ms, axis=1), dy_blocks))
                krow = krow + dot(jnp.concatenate(ks, axis=1), hot_ref[Q * first : Q * (first + 2), :])
            d_state = ds_state[:, cols]
            dsb = d_state.astype(BF)
            startb = start_ref[0, :, cols]
            tail_e = dot(tail_2, ee)
            from_state = tail_e * dot(bm, dsb)
            du = jnp.concatenate(parts, axis=1) + from_state
            edy = dot(ex_2, ee) * dy
            edyb = edy.astype(BF)
            d_b = d_b + dot_nt((tail_e * u).astype(BF), dsb)
            d_c = d_c + dot_nt(edyb, startb)
            three = jnp.concatenate([edy * dot(cm, startb), u * from_state, x * du], axis=0).astype(BF)
            sums = sums + dot(three, er_ref[cols, :])
            rows = jnp.concatenate(
                [
                    jnp.sum(startb.astype(F32) * d_state, axis=0, keepdims=True),
                    jnp.sum(dy * x, axis=0, keepdims=True),
                    jnp.zeros((6, GROUP), F32),
                ],
                axis=0,
            )
            rows_hi = rows.astype(BF)
            rows_lo = (rows - rows_hi.astype(F32)).astype(BF)
            row_sums = row_sums + dot(jnp.concatenate([rows_hi, rows_lo], axis=0), er_ref[cols, :])
            ds_state[:, cols] = dot(end_2, ee)[0:1] * d_state + dot_tn(cm, edyb)
            conv_back(cols, (step_e * du + skip_ref[:, cols] * dy) * slope_ref[:, cols].astype(F32))

        d_mixb = jnp.where(causal, d_mix, 0.0).astype(BF)
        d_bc = jnp.concatenate([d_b + dot(d_mixb, cm), d_c + dot_tn(d_mixb, bm)], axis=1)
        conv_back(slice(di, cd), d_bc * slope_ref[:, di:].astype(F32))
        upper = causal.astype(F32)
        strict = tri(Q, Q, lambda r, c: c < r).astype(F32)
        row_sums = row_sums[0:8] + row_sums[8:16]
        d_decay = (
            dot(upper, kcol[...].T + sums[:Q] - krow, EXACT)
            + dot(strict, sums[Q : 2 * Q], EXACT)
            + at_end * row_sums[0:1]
        )
        d_dt = (sums[2 * Q :] + nega * d_decay) * sigmoid(dtv)
        d_ref[:, cd:] = d_dt.astype(BF)
        ghead_ref[0:1, :] += jnp.sum(d_dt, axis=0, keepdims=True)
        ghead_ref[1:2, :] += jnp.sum(d_decay * nega * step, axis=0, keepdims=True)
        ghead_ref[2:3, :] += row_sums[1:2]

    @pl.when(i == n)
    def _():
        full_d[0:Q, :] = jnp.zeros((Q, cd), BF)
        cin = prev_ref[...].astype(F32)
        edge = jnp.zeros((HALO, cd), F32)
        for k in range(CONV - 1):
            later = dot(shift_ref[Q * (k + 1) - HALO : Q * (k + 1), :], full_d[...])
            edge = edge + tap(k) * later
            gconv_ref[k : k + 1, :] += jnp.sum(later * cin, axis=0, keepdims=True)
        d_ref[...] = jnp.zeros_like(d_ref)
        d_ref[Q - HALO :, :cd] = edge.astype(BF)


def stream_back_kernel(d_ref, dnz_ref, wa_ref, wb_ref, small_ref, s_ref, halo_ref, cot_ref, gs_ref, msg_ref):
    i = pl.program_id(0)
    d, ca = wa_ref.shape
    cdp = d_ref.shape[1]

    def through(dn, s):
        inv = root_of(s)
        weighted = small_ref[0:1, :d] * dn
        unit = s * inv
        return inv * (weighted - unit * jnp.mean(weighted * unit, axis=-1, keepdims=True))

    def back(rows):
        return dot_nt(rows[:, :ca], wa_ref[...]) + dot_nt(rows[:, ca:], wb_ref[:, : cdp - ca])

    @pl.when(i == 0)
    def _():
        msg_ref[...] = through(back(d_ref[Q - HALO :, :]), halo_ref[...])

    @pl.when(i > 0)
    def _():
        gs_ref[...] = cot_ref[...] + through(dnz_ref[...] + back(d_ref[...]), s_ref[...])


VMEM = pltpu.CompilerParams(vmem_limit_bytes=60 * 2**20)


def whole(a):
    return pl.BlockSpec(a.shape, lambda *_: (0,) * a.ndim)


def cost(flops, *arrays):
    return pl.CostEstimate(
        flops=int(flops), transcendentals=0, bytes_accessed=sum(a.size * a.dtype.itemsize for a in arrays)
    )


def shape(*dims, dtype=F32):
    return jax.ShapeDtypeStruct(dims, dtype)


def flip(v, axis, n, bit):
    return lax.ppermute(v, axis, [(s, s ^ bit) for s in range(n)])


def shift(v, axis, n, by):
    return lax.ppermute(v, axis, [(s, (s + by) % n) for s in range(n)])


def far_gather(v, n):
    far = n // 4
    z = lax.axis_index("seq") // 4
    got = [v] + [shift(v, "seq", n, 4 * k) for k in range(1, far)]
    buf = jnp.zeros((far,) + v.shape, v.dtype)
    for k in range(far):
        buf = lax.dynamic_update_slice_in_dim(buf, got[k][None], (z - k) % far, 0)
    return buf


def pair_gather(v, n, bit, axis):
    other = flip(v, "seq", n, bit)
    mine = (lax.axis_index("seq") // bit) % 2 == 0
    return jnp.where(mine, jnp.stack([v, other], axis), jnp.stack([other, v], axis))


def gather_rows(v, n, ca):
    a, b = v[:, :ca], v[:, ca:]
    b = pair_gather(b, n, 2, 0)
    a = far_gather(a, n)
    a = pair_gather(a, n, 2, 1)
    b = far_gather(b, n)
    a, b = pair_gather(a, n, 1, 2), pair_gather(b, n, 1, 2)
    return a.reshape(-1, a.shape[-1]), b.reshape(-1, b.shape[-1])


def pair_scatter(v, n, bit, axis):
    me = (lax.axis_index("seq") // bit) % 2
    mine = lax.dynamic_index_in_dim(v, me, axis, False)
    other = flip(lax.dynamic_index_in_dim(v, 1 - me, axis, False), "seq", n, bit)
    return (mine.astype(F32) + other.astype(F32)).astype(BF)


def far_scatter(v, n):
    far = n // 4
    z = lax.axis_index("seq") // 4
    total = lax.dynamic_index_in_dim(v, z, 0, False).astype(F32)
    for k in range(1, far):
        sent = lax.dynamic_index_in_dim(v, (z + k) % far, 0, False)
        total = total + shift(sent, "seq", n, 4 * k).astype(F32)
    return total.astype(BF)


def over_hx(v, hx):
    if hx == 2:
        b = v.astype(BF)
        return b.astype(F32) + flip(b, "hx", hx, 1).astype(F32)
    return lax.psum(v.astype(F32), "hx")


def sum_steps(n, hx):
    steps = []
    for axis, size in (("seq", n), ("hx", hx)):
        bit = 1
        while bit < size:
            steps.append(functools.partial(lambda axis, size, bit, v: v + flip(v, axis, size, bit), axis, size, bit))
            bit *= 2
    return steps


def together(*values):
    return lax.optimization_barrier(values)


def shards(
    stream,
    cotangent,
    norm_gain,
    in_main,
    in_dt,
    conv_weight,
    conv_bias,
    dt_bias,
    a_log,
    skip_gain,
    gated_gain,
    out_weight,
):
    n, hx = lax.axis_size("seq"), lax.axis_size("hx")
    s, cot = stream[0], cotangent[0]
    t, d = s.shape
    heads = in_dt.shape[1]
    di = out_weight.shape[0] * n
    cd = conv_weight.shape[1] * n
    width = di // heads
    nc = t // Q
    cdp = cd + LANES
    rows = in_main.shape[0]
    per = di // d

    def lanes(v):
        return jnp.pad(v, ((0, 0), (0, LANES - v.shape[1])))

    small = jnp.concatenate(
        [lanes(norm_gain[None]), lanes(conv_weight), lanes(conv_bias[None]), lanes(gated_gain[None])], axis=0
    )
    small = jnp.pad(small, ((0, rows - small.shape[0]), (0, 0)))
    wx = jnp.concatenate([in_main[:, di:], lanes(in_dt), small], axis=1)
    ca = wx.shape[1] * 2 // 3 // GROUP * GROUP
    wa, wb = gather_rows(wx, n, ca)
    wzo = jnp.concatenate([in_main[:, :di], out_weight.reshape(per, rows, d).transpose(1, 0, 2).reshape(rows, di)], axis=1)
    wzo = lax.all_gather(wzo, "seq", axis=0, tiled=True)
    halo = lax.ppermute(s[t - HALO :], "hx", [(r, r + 1) for r in range(hx - 1)])

    head_rows = jnp.pad(jnp.stack([dt_bias, -jnp.exp(a_log)]), ((0, 6), (0, LANES - heads)))
    owner = jnp.arange(di, dtype=jnp.int32) // width
    er = (owner[:, None] == jnp.arange(LANES, dtype=jnp.int32)[None, :]).astype(BF)
    one = (jnp.arange(LANES, dtype=jnp.int32)[:, None] == owner[None, :]).astype(BF)
    ee = jnp.concatenate([one, one], axis=0)
    skip = jnp.repeat(skip_gain, width)[None, :]
    hot = (
        (jnp.arange(heads * Q, dtype=jnp.int32) // Q)[:, None] == jnp.arange(LANES, dtype=jnp.int32)[None, :]
    ).astype(BF)

    block = jnp.arange(heads * Q, dtype=jnp.int32) // Q
    which = jnp.arange(LANES, dtype=jnp.int32)
    pick = ((which[:, None] % 32 == block[None, :]) & (which[:, None] < 96)).astype(BF)
    row = jnp.arange((CONV - 1) * Q, dtype=jnp.int32)[:, None]
    col = jnp.arange(Q + HALO, dtype=jnp.int32)[None, :]
    ahead = (col == HALO + row % Q - (CONV - 1) + row // Q).astype(BF)
    behind = (col == row % Q + (CONV - 1) - row // Q).astype(BF)
    nw = t // WIDE
    two = WIDE // Q

    def at(i):
        return jnp.maximum(i - 1, 0)

    wa, er, ee, skip, hot, pick, ahead, behind = together(wa, er, ee, skip, hot, pick, ahead, behind)
    args = (halo, s, wa, wb, head_rows, ee, ahead)
    nrm, cin, xc, slope, dtv, cum, base, sloc, fin, tot, small = pl.pallas_call(
        functools.partial(project_kernel, n),
        grid=(nw + 1,),
        in_specs=[whole(halo), pl.BlockSpec((WIDE, d), lambda i: (at(i), 0))] + [whole(a) for a in args[2:]],
        out_specs=[
            pl.BlockSpec((WIDE, d), lambda i: (i, 0)),
            pl.BlockSpec((WIDE, cd), lambda i: (i, 0)),
            pl.BlockSpec((WIDE, cd), lambda i: (at(i), 0)),
            pl.BlockSpec((WIDE, cd), lambda i: (at(i), 0)),
            pl.BlockSpec((WIDE, LANES), lambda i: (at(i), 0)),
            pl.BlockSpec((WIDE, LANES), lambda i: (at(i), 0)),
            pl.BlockSpec((8 * two, LANES), lambda i: (at(i), 0)),
            pl.BlockSpec((two, STATE, di), lambda i: (at(i), 0, 0)),
            pl.BlockSpec((STATE, di), lambda i: (0, 0)),
            pl.BlockSpec((8, LANES), lambda i: (0, 0)),
            pl.BlockSpec((8, cd), lambda i: (0, 0)),
        ],
        out_shape=[
            shape(t + WIDE, d, dtype=BF),
            shape(t + WIDE, cd, dtype=BF),
            shape(t, cd, dtype=BF),
            shape(t, cd, dtype=BF),
            shape(t, LANES),
            shape(t, LANES),
            shape(8 * nc, LANES),
            shape(nc, STATE, di, dtype=BF),
            shape(STATE, di, dtype=BF),
            shape(8, LANES),
            shape(8, cd),
        ],
        scratch_shapes=[pltpu.VMEM((WIDE + HALO, cd), BF), pltpu.VMEM((STATE, di), F32), pltpu.VMEM((8, LANES), F32)],
        compiler_params=VMEM,
        cost_estimate=cost(3 * t * d * cdp, s, wa, wb, s, s),
        name="project",
    )(*args)

    def carry(v, step_by):
        links = [(r, r + step_by) for r in range(hx) if 0 <= r + step_by < hx]
        got = lax.ppermute(v, "hx", links)
        total = got
        if hx > 2:
            fade = jnp.repeat(jnp.exp(tot[0, :heads]), width)[None, :]
            total = got.astype(F32)
            for _ in range(hx - 2):
                got = lax.ppermute((fade * got.astype(F32)).astype(BF), "hx", links)
                total = total + got.astype(F32)
            total = total.astype(BF)
        return total

    hin = carry(fin, 1)

    args = (xc, dtv, cum, skip, ee, pick)
    yi = pl.pallas_call(
        functools.partial(intra_kernel, width),
        grid=(nc,),
        in_specs=[
            pl.BlockSpec((Q, cd), lambda i: (i, 0)),
            pl.BlockSpec((Q, LANES), lambda i: (i, 0)),
            pl.BlockSpec((Q, LANES), lambda i: (i, 0)),
            whole(skip),
            whole(ee),
            whole(pick),
        ],
        out_specs=pl.BlockSpec((Q, di), lambda i: (i, 0)),
        out_shape=shape(t, di, dtype=BF),
        scratch_shapes=[pltpu.VMEM(pick.shape, BF)],
        compiler_params=VMEM,
        cost_estimate=cost(2 * t * d * di, xc, xc),
        name="intra",
    )(*args)

    args = (yi, nrm, xc, cum, base, sloc, hin, s, cot, wzo, small, ee)
    out, mixed, dsc, dz, start, gst = pl.pallas_call(
        functools.partial(gate_kernel, n),
        grid=(nw,),
        in_specs=[
            pl.BlockSpec((WIDE, di), lambda i: (i, 0)),
            pl.BlockSpec((WIDE, d), lambda i: (i + 1, 0)),
            pl.BlockSpec((WIDE, STATE), lambda i: (i, cd // STATE - 1)),
            pl.BlockSpec((WIDE, LANES), lambda i: (i, 0)),
            pl.BlockSpec((8 * two, LANES), lambda i: (i, 0)),
            pl.BlockSpec((two, STATE, di), lambda i: (i, 0, 0)),
            whole(hin),
            pl.BlockSpec((WIDE, d), lambda i: (i, 0)),
            pl.BlockSpec((WIDE, d), lambda i: (i, 0)),
            whole(wzo),
            whole(small),
            whole(ee),
        ],
        out_specs=[
            pl.BlockSpec((WIDE, d), lambda i: (i, 0)),
            pl.BlockSpec((WIDE, di), lambda i: (i, 0)),
            pl.BlockSpec((WIDE, di), lambda i: (i, 0)),
            pl.BlockSpec((WIDE, di), lambda i: (i, 0)),
            pl.BlockSpec((two, STATE, di), lambda i: (i, 0, 0)),
            pl.BlockSpec((STATE, di), lambda i: (0, 0)),
        ],
        out_shape=[
            shape(t, d),
            shape(t, di, dtype=BF),
            shape(t, di, dtype=BF),
            shape(t, di, dtype=BF),
            shape(nc, STATE, di, dtype=BF),
            shape(STATE, di, dtype=BF),
        ],
        scratch_shapes=[
            pltpu.VMEM((STATE, di), F32),
            pltpu.VMEM((di, d), BF),
            pltpu.VMEM((WIDE, di), BF),
            pltpu.VMEM((WIDE, di), F32),
            pltpu.VMEM((WIDE, di), F32),
        ],
        compiler_params=VMEM,
        cost_estimate=cost(6 * t * d * di, yi, yi, yi, xc, s, s, s),
        name="gate",
    )(*args)

    gin = carry(gst, -1)
    g_z = dot_tn(nrm[WIDE:], dz).astype(BF)
    g_out = dot_tn(mixed, cot.astype(BF)).astype(BF)
    g_zo = jnp.concatenate([g_z, g_out.reshape(n, per, rows, d).transpose(0, 2, 1, 3).reshape(d, di)], axis=1)
    g_zo = lax.psum_scatter(g_zo, "seq", scatter_dimension=0, tiled=True)
    args = (xc, slope, dtv, cum, start, gin, dsc, cin, cin, small, head_rows, skip, ee, er, hot, pick, behind)

    def back(i):
        return jnp.maximum(nc - 1 - i, 0)

    dx, gconv, ghead = pl.pallas_call(
        functools.partial(scan_back_kernel, width),
        grid=(nc + 1,),
        in_specs=[
            pl.BlockSpec((Q, cd), lambda i: (back(i), 0)),
            pl.BlockSpec((Q, cd), lambda i: (back(i), 0)),
            pl.BlockSpec((Q, LANES), lambda i: (back(i), 0)),
            pl.BlockSpec((Q, LANES), lambda i: (back(i), 0)),
            pl.BlockSpec((1, STATE, di), lambda i: (back(i), 0, 0)),
            whole(gin),
            pl.BlockSpec((Q, di), lambda i: (back(i), 0)),
            pl.BlockSpec((Q, cd), lambda i: (back(i) + two, 0)),
            pl.BlockSpec((HALO, cd), lambda i: (WIDE // HALO - 1, 0)),
        ]
        + [whole(a) for a in args[9:]],
        out_specs=[
            pl.BlockSpec((Q, cdp), lambda i: (nc - i, 0)),
            pl.BlockSpec((8, cd), lambda i: (0, 0)),
            pl.BlockSpec((8, LANES), lambda i: (0, 0)),
        ],
        out_shape=[shape(t + Q, cdp, dtype=BF), shape(8, cd), shape(8, LANES)],
        scratch_shapes=[
            pltpu.VMEM((Q + HALO, cd), BF),
            pltpu.VMEM((STATE, di), F32),
            pltpu.VMEM((LANES, Q), F32),
            pltpu.VMEM(pick.shape, BF),
        ],
        compiler_params=VMEM,
        cost_estimate=cost(8 * t * d * di, xc, xc, xc, xc),
        name="scan_back",
    )(*args)

    packed = jnp.concatenate([gconv, jnp.pad(ghead, ((0, 0), (0, LANES)))], axis=1)
    steps = sum_steps(n, hx)
    g_x = dot_tn(nrm[WIDE - Q :], dx).astype(BF)
    g_x, dz, packed = together(g_x, dz, packed)
    g_x = pair_scatter(g_x.reshape(n // 4, 2, 2, rows, cdp), n, 1, 2)
    packed = steps[0](packed)
    dnz = dot_nt(dz, wzo[:, :di])
    g_x, packed, dnz, dx = together(g_x, packed, dnz, dx)
    g_x = pair_scatter(g_x, n, 2, 1)
    packed = steps[1](packed)

    args = (dx, dnz, wa, wb, small, s, halo, cot)
    g_stream, msg = pl.pallas_call(
        stream_back_kernel,
        grid=(nc + 1,),
        in_specs=[
            pl.BlockSpec((Q, cdp), lambda i: (i, 0)),
            pl.BlockSpec((Q, d), lambda i: (at(i), 0)),
            whole(wa),
            whole(wb),
            whole(small),
            pl.BlockSpec((Q, d), lambda i: (at(i), 0)),
            whole(halo),
            pl.BlockSpec((Q, d), lambda i: (at(i), 0)),
        ],
        out_specs=[pl.BlockSpec((Q, d), lambda i: (at(i), 0)), pl.BlockSpec((HALO, d), lambda i: (0, 0))],
        out_shape=[shape(t, d), shape(HALO, d)],
        compiler_params=VMEM,
        cost_estimate=cost(2 * t * d * cdp, s, s, s, s, wa, wb),
        name="stream_back",
    )(*args)
    g_x, packed, msg, g_zo = together(g_x, packed, msg, g_zo)
    g_zo = over_hx(g_zo, hx)
    g_x = far_scatter(g_x, n)
    for step in steps[2:-1]:
        packed = step(packed)
    msg = lax.ppermute(msg, "hx", [(r + 1, r) for r in range(hx - 1)])
    g_x, packed, msg, g_zo = together(g_x, packed, msg, g_zo)
    g_x = over_hx(g_x, hx)
    packed = steps[-1](packed)
    g_stream = lax.dynamic_update_slice(g_stream, g_stream[t - HALO :] + msg, (t - HALO, 0))
    mine = lax.dynamic_slice_in_dim(packed[:, :cd], lax.axis_index("seq") * (cd // n), cd // n, 1)
    g_z, g_out = g_zo[:, :di], g_zo[:, di:].reshape(rows, per, d).transpose(1, 0, 2).reshape(rows * per, d)
    g_main = jnp.concatenate([g_z, g_x[:, :cd]], axis=1)
    g_dt = g_x[:, cd : cd + heads]
    g_norm = (
        jnp.sum(in_main.astype(F32) * g_main, axis=1) + jnp.sum(in_dt.astype(F32) * g_dt, axis=1)
    ) / norm_gain.astype(F32)
    g_gate = jnp.sum(out_weight.astype(F32) * g_out, axis=1) / gated_gain.astype(F32)
    return (
        out[None],
        g_stream[None],
        g_norm,
        g_main,
        g_dt,
        mine[:CONV],
        mine[CONV],
        packed[0, cd : cd + heads],
        packed[1, cd : cd + heads],
        packed[2, cd : cd + heads],
        g_gate,
        g_out,
    )


def solution(mesh):
    placed = (
        P("seq", "hx", None),
        P("seq", "hx", None),
        P("seq"),
        P("seq", None),
        P("seq", None),
        P(None, "seq"),
        P("seq"),
        P(),
        P(),
        P(),
        P("seq"),
        P("seq", None),
    )
    return jax.shard_map(
        shards,
        mesh=mesh,
        in_specs=placed,
        out_specs=(
            P("seq", "hx", None),
            P("seq", "hx", None),
            P("seq"),
            P("seq", None),
            P("seq", None),
            P(None, "seq"),
            P("seq"),
            P(),
            P(),
            P(),
            P("seq"),
            P("seq", None),
        ),
        check_vma=False,
    )
```

profile of v0, /device:TPU:0, one launch (start us, length us, event | category | flops | bytes accessed | tf_op | source)
XLA Modules:
  0.0 290.7 jit_solution(17377032233439151666)
XLA Ops:
  8.2 3.1 %collective-permute-start.1 = (bf16[48,1280]{1,0:T(8,128)(2,1)S(1)}, bf16[48,1280]{1,0:T(8,128)(2,1)S(1)}, u32[]{:S(2)}, u32[]{:S(2)}) collective-permute-start(bf16[48,1280]{1,0:T(8,128)(2,1)S(1)} %slice.63), channel_id=1, source_target_pairs={{0,8},{2,10},{4,12},{6,14},{8,16},{10,18},{12,20},{14,22},{16,24},... | collective-permute-start | bytes 368648 | tf_op jit(solution)/shard_map/ppermute | solution.py:540
  11.3 2.6 collective-permute-start.2
  13.9 1.3 collective-permute-start.3
  17.7 1.6 collective-permute-start.6
  20.1 3.4 %collective-permute-start = (f32[16,768]{1,0:T(8,128)S(1)}, f32[16,768]{1,0:T(8,128)S(1)}, u32[]{:S(2)}, u32[]{:S(2)}) collective-permute-start(f32[16,768]{1,0:T(8,128)S(1)} %slice_bitcast_fusion), channel_id=1, source_target_pairs={{0,1},{2,3},{4,5},{6,7},{8,9},{10,11},{12,13},{14,15},{16,17},{18,... | collective-permute-start | bytes 147464 | tf_op jit(solution)/shard_map/ppermute | solution.py:645
  24.4 1.0 copy.38
  30.0 1.0 fusion.8.er_ref
  31.0 2.1 fusion.6.hot_ref
  33.1 1.2 and_convert_fusion.pick_ref
  36.2 2.9 collective-permute-start.9
  39.7 6.7 %collective-permute-done.7 = bf16[2,48,768]{2,1,0:T(8,128)(2,1)S(1)} collective-permute-done((bf16[2,48,768]{2,1,0:T(8,128)(2,1)S(1)}, bf16[2,48,768]{2,1,0:T(8,128)(2,1)S(1)}, u32[]{:S(2)}, u32[]{:S(2)}) %collective-permute-start.7) | collective-permute-done | bytes 147488 | tf_op jit(solution)/shard_map/ppermute | solution.py:540
  46.5 7.8 %collective-permute-done.8 = bf16[2,48,768]{2,1,0:T(8,128)(2,1)S(1)} collective-permute-done((bf16[2,48,768]{2,1,0:T(8,128)(2,1)S(1)}, bf16[2,48,768]{2,1,0:T(8,128)(2,1)S(1)}, u32[]{:S(2)}, u32[]{:S(2)}) %collective-permute-start.8) | collective-permute-done | bytes 147488 | tf_op jit(solution)/shard_map/ppermute | solution.py:540
  55.3 1.0 collective-permute-done.10
  56.3 1.1 maximum_select_fusion.1
  57.7 1.5 maximum_select_fusion
  59.9 22.7 %project.1 = (bf16[1280,768]{1,0:T(8,128)(2,1)}, bf16[1280,1792]{1,0:T(8,128)(2,1)}, bf16[1024,1792]{1,0:T(8,128)(2,1)}, bf16[1024,1792]{1,0:T(8,128)(2,1)}, f32...) custom-call(f32[16,768]{1,0:T(8,128)} %copy-done.10, ...), custom_call_target="tpu_custom_call" | custom-call | flops 4529848320 | bytes 12582912 | tf_op jit(solution)/shard_map/project/pallas_call | solution.py:672
  82.6 3.0 %collective-permute-start.11 = (bf16[128,1536]{1,0:T(8,128)(2,1)}, bf16[128,1536]{1,0:T(8,128)(2,1)S(1)}, u32[]{:S(2)}, u32[]{:S(2)}) collective-permute-start(bf16[128,1536]{1,0:T(8,128)(2,1)} %get-tuple-element.67), channel_id=1, source_target_pairs={{0,1},{2,3},{4,5},{6,7},{8,9},{10,11},{12,13},{14,15},{16,17},{18,... | collective-permute-start | bytes 1179656 | tf_op jit(solution)/shard_map/ppermute | solution.py:710
  85.6 13.9 %intra.1.yi_ref = bf16[1024,1536]{1,0:T(8,128)(2,1)} custom-call(bf16[1024,1792]{1,0:T(8,128)(2,1)} %get-tuple-element.59.xc_ref.c_ref, f32[1024,128]{1,0:T(8,128)} %get-tuple-element.60.dtv_ref, f32[1024,128]{1,0:T(8,128)} %get-tuple-element.61.cum_ref, f32[1,1536]{1,0:T(1,128)} %broadcast_in_dim_reshape.3.skip_ref, ...), custom_call_target="tpu_custom_call" | custom-call | flops 2415919104 | bytes 7340032 | tf_op jit(solution)/shard_map/intra/pallas_call | solution.py:724
  100.2 27.3 %gate.1 = (f32[1024,768]{1,0:T(8,128)}, bf16[1024,1536]{1,0:T(8,128)(2,1)}, bf16[1024,1536]{1,0:T(8,128)(2,1)}, bf16[1024,1536]{1,0:T(8,128)(2,1)}, bf16[8,128,1...) custom-call(bf16[1024,1536]{1,0:T(8,128)(2,1)} %intra.1.yi_ref, bf16[1280,768]{1,0:T(8,128)(2,1)} %get-tuple-element.64.nrm_ref, ...), custom_call_target="tpu_custom_call" | custom-call | flops 7247757312 | bytes 22544384 | tf_op jit(solution)/shard_map/gate/pallas_call | solution.py:744
  127.6 4.9 %convolution_convert_fusion.1 = bf16[768,1536]{1,0:T(8,128)(2,1)S(1)} fusion(bf16[1024,1536]{1,0:T(8,128)(2,1)} %get-tuple-element.84, bf16[1280,768]{1,0:T(8,128)(2,1)S(1)} %copy-done.21), kind=kOutput, calls=%fused_computation.2 | convolution fusion | flops 2417098752 | bytes 7077888 | tf_op jit(solution)/shard_map/dot_general | solution.py:34
  132.5 3.0 %fusion.51 = bf16[1536,768]{1,0:T(8,128)(2,1)S(1)} fusion(bf16[1024,1536]{1,0:T(8,128)(2,1)S(1)} %copy-done.20, f32[1,1024,768]{2,1,0:T(8,128)S(1)} %copy-done.1), kind=kOutput, calls=%fused_computation.127 | convolution fusion | flops 2415919104 | bytes 8650752 | tf_op jit(solution)/shard_map/dot_general | solution.py:34
  135.5 2.2 copy.40
  138.1 2.8 pad_maximum_fusion
  140.9 1.0 copy-done.15
  141.9 1.5 collective-permute-start.12
  143.4 11.2 %collective-permute-done.12.gin_ref = bf16[128,1536]{1,0:T(8,128)(2,1)S(1)} collective-permute-done((bf16[128,1536]{1,0:T(8,128)(2,1)S(1)}, bf16[128,1536]{1,0:T(8,128)(2,1)S(1)}, u32[]{:S(2)}, u32[]{:S(2)}) %collective-permute-start.12) | collective-permute-done | bytes 393248 | tf_op jit(solution)/shard_map/ppermute | solution.py:710
  155.4 44.7 %scan_back.1 = (bf16[1152,1920]{1,0:T(8,128)(2,1)}, f32[8,1792]{1,0:T(8,128)}, f32[8,128]{1,0:T(8,128)}) custom-call(bf16[1024,1792]{1,0:T(8,128)(2,1)} %get-tuple-element.59.xc_ref.c_ref, bf16[1024,1792]{1,0:T(8,128)(2,1)} %get-tuple-element.70.slope_ref, f32[1024,128]{1,0:T(8,128)} %get-tuple-element.60.dtv_ref, f32[1024,128]{1,0:T(8,128)} %get-tuple-element.61.cum_ref, ...), custom_call_target="tpu_custom_call" | custom-call | flops 9663676416 | bytes 14680064 | tf_op jit(solution)/shard_map/scan_back/pallas_call | solution.py:799
  201.0 6.9 %convolution_convert_fusion.2 = bf16[768,1920]{1,0:T(8,128)(2,1)S(1)} fusion(bf16[1152,1920]{1,0:T(8,128)(2,1)} %get-tuple-element.85.d_ref, bf16[1280,768]{1,0:T(8,128)(2,1)S(1)} %copy-done.21), kind=kOutput, calls=%fused_computation.3 | convolution fusion | flops 3398860800 | bytes 9142272 | tf_op jit(solution)/shard_map/dot_general | solution.py:34
  207.9 1.6 copy-done.2
  210.2 7.2 %fusion.1.dnz_ref = f32[1024,768]{1,0:T(8,128)} fusion(bf16[1024,1536]{1,0:T(8,128)(2,1)} %get-tuple-element.84, bf16[768,3072]{1,0:T(8,128)(2,1)} %all-gather.2.cloned.1.call-done.wzo_ref), kind=kOutput, calls=%fused_computation.6 | convolution fusion | flops 2415919104 | bytes 8650752 | tf_op jit(solution)/shard_map/dot_general | solution.py:30
  217.9 1.3 collective-permute-start.15
  220.0 14.8 %stream_back.1 = (f32[1024,768]{1,0:T(8,128)}, f32[16,768]{1,0:T(8,128)}) custom-call(bf16[1152,1920]{1,0:T(8,128)(2,1)} %get-tuple-element.85.d_ref, f32[1024,768]{1,0:T(8,128)} %fusion.1.dnz_ref, bf16[768,1280]{1,0:T(8,128)(2,1)} %bitcast.103, bf16[768,768]{1,0:T(8,128)(2,1)} %bitcast.105, f32[8,1792]{1,0:T(8,128)} %get-tuple-element.68.small_ref, ...), custom_call_target="tpu_custom_call" | custom-call | flops 3019898880 | bytes 15728640 | tf_op jit(solution)/shard_map/stream_back/pallas_call | solution.py:843
  234.8 3.0 %collective-permute-done.16 = f32[8,2048]{1,0:T(8,128)S(1)} collective-permute-done((f32[8,2048]{1,0:T(8,128)S(1)}, f32[8,2048]{1,0:T(8,128)S(1)}, u32[]{:S(2)}, u32[]{:S(2)}) %collective-permute-start.16) | collective-permute-done | bytes 65568 | tf_op jit(solution)/shard_map/ppermute | solution.py:536
  238.9 3.5 %collective-permute-start.17 = (bf16[48,1920]{1,0:T(8,128)(2,1)}, bf16[48,1920]{1,0:T(8,128)(2,1)}, u32[]{:S(2)}, u32[]{:S(2)}) collective-permute-start(bf16[48,1920]{1,0:T(8,128)(2,1)} %get-tuple-element.128), channel_id=1, source_target_pairs={{0,8},{2,10},{4,12},{6,14},{8,16},{10,18},{12,20},{14,22},{16,24},... | collective-permute-start | bytes 552968 | tf_op jit(solution)/shard_map/ppermute | solution.py:540
  242.4 1.0 collective-permute-start.18
  243.4 1.4 collective-permute-start.19
  245.5 10.8 %collective-permute-done.20 = f32[8,2048]{1,0:T(8,128)S(1)} collective-permute-done((f32[8,2048]{1,0:T(8,128)S(1)}, f32[8,2048]{1,0:T(8,128)S(1)}, u32[]{:S(2)}, u32[]{:S(2)}) %collective-permute-start.20) | collective-permute-done | bytes 65568 | tf_op jit(solution)/shard_map/ppermute | solution.py:536
  257.0 1.9 copy.58
  258.9 2.7 collective-permute-done.21
  261.7 1.3 collective-permute-start.22
  263.9 2.0 fusion.13
  265.8 1.4 collective-permute-done.23
  268.6 1.1 collective-permute-start.24
  270.6 1.9 reshape.320
  272.5 1.0 copy.42
  273.5 1.1 multiply_reduce_fusion.1
  278.7 1.1 convert_add_fusion.4
  281.3 2.0 multiply_reduce_fusion
  (139 shorter events, 30.4 us)
Async XLA Ops:
  7.2 22.8 %copy-start.5 = (bf16[48,3328]{1,0:T(8,128)(2,1)S(1)}, bf16[48,3328]{1,0:T(8,128)(2,1)}, u32[]{:S(2)}) copy-start(bf16[48,3328]{1,0:T(8,128)(2,1)} %param.15) | copy-start | bytes 958468
  7.2 19.3 %copy-start.12 = (f32[24]{0:T(128)S(1)}, f32[24]{0:T(128)}, u32[]{:S(2)}) copy-start(f32[24]{0:T(128)} %param.21) | copy-start | bytes 292
  7.2 20.0 %copy-start.19 = (f32[24]{0:T(128)S(1)}, f32[24]{0:T(128)}, u32[]{:S(2)}) copy-start(f32[24]{0:T(128)} %param.20) | copy-start | bytes 292
  7.2 92.2 %all-gather.2.cloned.1.call-start = ((), (), s32[]{:S(2)}) async-start(), calls=%async_computation.1 | async-start | bytes 5013504 | tf_op jit(solution)/shard_map/all_gather | solution.py:644
  8.2 27.5 %collective-permute-start.1 = (bf16[48,1280]{1,0:T(8,128)(2,1)S(1)}, bf16[48,1280]{1,0:T(8,128)(2,1)S(1)}, u32[]{:S(2)}, u32[]{:S(2)}) collective-permute-start(bf16[48,1280]{1,0:T(8,128)(2,1)S(1)} %slice.63), channel_id=1, source_target_pairs={{0,8},{2,10},{4,12},{6,14},{8,16},{10,18},{12,20},{14,22},{16,24},... | collective-permute-start | bytes 368648 | tf_op jit(solution)/shard_map/ppermute | solution.py:540
  11.3 24.9 %collective-permute-start.2 = (bf16[48,1280]{1,0:T(8,128)(2,1)S(1)}, bf16[48,1280]{1,0:T(8,128)(2,1)S(1)}, u32[]{:S(2)}, u32[]{:S(2)}) collective-permute-start(bf16[48,1280]{1,0:T(8,128)(2,1)S(1)} %slice.63), channel_id=1, source_target_pairs={{0,16},{2,18},{4,20},{6,22},{8,24},{10,26},{12,28},{14,30},{16,0},... | collective-permute-start | bytes 368648 | tf_op jit(solution)/shard_map/ppermute | solution.py:540
  13.9 25.2 %collective-permute-start.3 = (bf16[48,1280]{1,0:T(8,128)(2,1)S(1)}, bf16[48,1280]{1,0:T(8,128)(2,1)S(1)}, u32[]{:S(2)}, u32[]{:S(2)}) collective-permute-start(bf16[48,1280]{1,0:T(8,128)(2,1)S(1)} %slice.63), channel_id=1, source_target_pairs={{0,24},{2,26},{4,28},{6,30},{8,0},{10,2},{12,4},{14,6},{16,8},{18,... | collective-permute-start | bytes 368648 | tf_op jit(solution)/shard_map/ppermute | solution.py:540
  17.7 17.2 %collective-permute-start.6 = (bf16[48,768]{1,0:T(8,128)(2,1)S(1)}, bf16[48,768]{1,0:T(8,128)(2,1)S(1)}, u32[]{:S(2)}, u32[]{:S(2)}) collective-permute-start(bf16[48,768]{1,0:T(8,128)(2,1)S(1)} %fusion.21), channel_id=1, source_target_pairs={{0,4},{2,6},{4,0},{6,2},{8,12},{10,14},{12,8},{14,10},{16,20},{18,... | collective-permute-start | bytes 221192 | tf_op jit(solution)/shard_map/ppermute | solution.py:536
  20.1 39.2 %collective-permute-start = (f32[16,768]{1,0:T(8,128)S(1)}, f32[16,768]{1,0:T(8,128)S(1)}, u32[]{:S(2)}, u32[]{:S(2)}) collective-permute-start(f32[16,768]{1,0:T(8,128)S(1)} %slice_bitcast_fusion), channel_id=1, source_target_pairs={{0,1},{2,3},{4,5},{6,7},{8,9},{10,11},{12,13},{14,15},{16,17},{18,... | collective-permute-start | bytes 147464 | tf_op jit(solution)/shard_map/ppermute | solution.py:645
  25.4 8.9 %copy-start.13 = (f32[24]{0:T(128)S(1)}, f32[24]{0:T(128)}, u32[]{:S(2)}) copy-start(f32[24]{0:T(128)} %param.19) | copy-start | bytes 292
  26.2 211.8 %reduce-scatter.2.cloned.1.call-start = ((), (), s32[]{:S(2)}) async-start(), calls=%async_computation.2 | async-start | bytes 5013504 | tf_op jit(solution)/shard_map/reduce_scatter | solution.py:793
  34.9 11.5 %collective-permute-start.7 = (bf16[2,48,768]{2,1,0:T(8,128)(2,1)S(1)}, bf16[2,48,768]{2,1,0:T(8,128)(2,1)S(1)}, u32[]{:S(2)}, u32[]{:S(2)}) collective-permute-start(bf16[2,48,768]{2,1,0:T(8,128)(2,1)S(1)} %maximum_select_fusion.4), channel_id=1, source_target_pairs={{0,8},{2,10},{4,12},{6,14},{8,16},{10,18},{12,20},{14,22},{16,24},... | collective-permute-start | bytes 442376 | tf_op jit(solution)/shard_map/ppermute | solution.py:540
  35.7 18.5 %collective-permute-start.8 = (bf16[2,48,768]{2,1,0:T(8,128)(2,1)S(1)}, bf16[2,48,768]{2,1,0:T(8,128)(2,1)S(1)}, u32[]{:S(2)}, u32[]{:S(2)}) collective-permute-start(bf16[2,48,768]{2,1,0:T(8,128)(2,1)S(1)} %maximum_select_fusion.4), channel_id=1, source_target_pairs={{0,16},{2,18},{4,20},{6,22},{8,24},{10,26},{12,28},{14,30},{16,0},... | collective-permute-start | bytes 442376 | tf_op jit(solution)/shard_map/ppermute | solution.py:540
  36.2 18.1 %collective-permute-start.9 = (bf16[2,48,768]{2,1,0:T(8,128)(2,1)S(1)}, bf16[2,48,768]{2,1,0:T(8,128)(2,1)S(1)}, u32[]{:S(2)}, u32[]{:S(2)}) collective-permute-start(bf16[2,48,768]{2,1,0:T(8,128)(2,1)S(1)} %maximum_select_fusion.4), channel_id=1, source_target_pairs={{0,24},{2,26},{4,28},{6,30},{8,0},{10,2},{12,4},{14,6},{16,8},{18,... | collective-permute-start | bytes 442376 | tf_op jit(solution)/shard_map/ppermute | solution.py:540
  39.1 15.2 %collective-permute-start.4 = (bf16[4,48,1280]{2,1,0:T(8,128)(2,1)S(1)}, bf16[4,48,1280]{2,1,0:T(8,128)(2,1)S(1)}, u32[]{:S(2)}, u32[]{:S(2)}) collective-permute-start(bf16[4,48,1280]{2,1,0:T(8,128)(2,1)S(1)} %bitcast_dynamic-update-slice_fusion.3), channel_id=1, source_target_pairs={{0,4},{2,6},{4,0},{6,2},{8,12},{10,14},{12,8},{14,10},{16,20},{18,... | collective-permute-start | bytes 1474568 | tf_op jit(solution)/shard_map/ppermute | solution.py:536
  54.3 2.1 collective-permute-start.10
  54.4 3.3 %collective-permute-start.5 = (bf16[4,2,48,1280]{3,2,1,0:T(8,128)(2,1)S(1)}, bf16[4,2,48,1280]{3,2,1,0:T(8,128)(2,1)S(1)}, u32[]{:S(2)}, u32[]{:S(2)}) collective-permute-start(bf16[4,2,48,1280]{3,2,1,0:T(8,128)(2,1)S(1)} %maximum_select_fusion.2), channel_id=1, source_target_pairs={{0,2},{2,0},{4,6},{6,4},{8,10},{10,8},{12,14},{14,12},{16,18},{18,... | collective-permute-start | bytes 2949128 | tf_op jit(solution)/shard_map/ppermute | solution.py:536
  82.6 16.9 %collective-permute-start.11 = (bf16[128,1536]{1,0:T(8,128)(2,1)}, bf16[128,1536]{1,0:T(8,128)(2,1)S(1)}, u32[]{:S(2)}, u32[]{:S(2)}) collective-permute-start(bf16[128,1536]{1,0:T(8,128)(2,1)} %get-tuple-element.67), channel_id=1, source_target_pairs={{0,1},{2,3},{4,5},{6,7},{8,9},{10,11},{12,13},{14,15},{16,17},{18,... | collective-permute-start | bytes 1179656 | tf_op jit(solution)/shard_map/ppermute | solution.py:710
  99.4 0.8 copy-start.17
  100.2 27.3 %copy-start.21 = (bf16[1280,768]{1,0:T(8,128)(2,1)S(1)}, bf16[1280,768]{1,0:T(8,128)(2,1)}, u32[]{:S(2)}) copy-start(bf16[1280,768]{1,0:T(8,128)(2,1)} %get-tuple-element.64.nrm_ref) | copy-start | bytes 5898244
  127.5 5.0 %copy-start.1 = (f32[1,1024,768]{2,1,0:T(8,128)S(1)}, f32[1,1024,768]{2,1,0:T(8,128)}, u32[]{:S(2)}) copy-start(f32[1,1024,768]{2,1,0:T(8,128)} %param.13) | copy-start | bytes 9437188
  127.5 4.9 %copy-start.20 = (bf16[1024,1536]{1,0:T(8,128)(2,1)S(1)}, bf16[1024,1536]{1,0:T(8,128)(2,1)}, u32[]{:S(2)}) copy-start(bf16[1024,1536]{1,0:T(8,128)(2,1)} %get-tuple-element.91) | copy-start | bytes 9437188
  140.9 1.0 copy-start.15
  141.9 12.8 %collective-permute-start.12 = (bf16[128,1536]{1,0:T(8,128)(2,1)S(1)}, bf16[128,1536]{1,0:T(8,128)(2,1)S(1)}, u32[]{:S(2)}, u32[]{:S(2)}) collective-permute-start(bf16[128,1536]{1,0:T(8,128)(2,1)S(1)} %copy-done.15), channel_id=1, source_target_pairs={{1,0},{3,2},{5,4},{7,6},{9,8},{11,10},{13,12},{15,14},{17,16},{19,... | collective-permute-start | bytes 1179656 | tf_op jit(solution)/shard_map/ppermute | solution.py:710
  207.9 1.6 copy-start.2
  209.6 7.8 %collective-permute-start.13 = (bf16[4,2,48,1920]{3,2,1,0:T(8,128)(2,1)S(1)}, bf16[4,2,48,1920]{3,2,1,0:T(8,128)(2,1)S(1)}, u32[]{:S(2)}, u32[]{:S(2)}) collective-permute-start(bf16[4,2,48,1920]{3,2,1,0:T(8,128)(2,1)S(1)} %dynamic-slice_bitcast_fusion), channel_id=1, source_target_pairs={{0,2},{2,0},{4,6},{6,4},{8,10},{10,8},{12,14},{14,12},{16,18},{18,... | collective-permute-start | bytes 4423688 | tf_op jit(solution)/shard_map/ppermute | solution.py:536
  209.7 7.7 %copy-start.3 = (bf16[768,1920]{1,0:T(8,128)(2,1)S(1)}, bf16[768,1920]{1,0:T(8,128)(2,1)}, u32[]{:S(2)}) copy-start(bf16[768,1920]{1,0:T(8,128)(2,1)} %copy-done.2) | copy-start | bytes 8847364
  209.7 7.7 %collective-permute-start.14 = (f32[8,2048]{1,0:T(8,128)S(1)}, f32[8,2048]{1,0:T(8,128)S(1)}, u32[]{:S(2)}, u32[]{:S(2)}) collective-permute-start(f32[8,2048]{1,0:T(8,128)S(1)} %select_maximum_fusion), channel_id=1, source_target_pairs={{0,2},{2,0},{4,6},{6,4},{8,10},{10,8},{12,14},{14,12},{16,18},{18,... | collective-permute-start | bytes 196616 | tf_op jit(solution)/shard_map/ppermute | solution.py:536
  217.9 19.8 %collective-permute-start.15 = (bf16[4,48,1920]{2,1,0:T(8,128)(2,1)S(1)}, bf16[4,48,1920]{2,1,0:T(8,128)(2,1)S(1)}, u32[]{:S(2)}, u32[]{:S(2)}) collective-permute-start(bf16[4,48,1920]{2,1,0:T(8,128)(2,1)S(1)} %dynamic-slice_bitcast_fusion.1), channel_id=1, source_target_pairs={{0,4},{2,6},{4,0},{6,2},{8,12},{10,14},{12,8},{14,10},{16,20},{18,... | collective-permute-start | bytes 2211848 | tf_op jit(solution)/shard_map/ppermute | solution.py:536
  219.2 18.5 %collective-permute-start.16 = (f32[8,2048]{1,0:T(8,128)S(1)}, f32[8,2048]{1,0:T(8,128)S(1)}, u32[]{:S(2)}, u32[]{:S(2)}) collective-permute-start(f32[8,2048]{1,0:T(8,128)S(1)} %add.260), channel_id=1, source_target_pairs={{0,4},{2,6},{4,0},{6,2},{8,12},{10,14},{12,8},{14,10},{16,20},{18,... | collective-permute-start | bytes 196616 | tf_op jit(solution)/shard_map/ppermute | solution.py:536
  238.0 19.0 %copy-start.4 = (bf16[4,48,1920]{2,1,0:T(8,128)(2,1)}, bf16[4,48,1920]{2,1,0:T(8,128)(2,1)S(1)}, u32[]{:S(2)}) copy-start(bf16[4,48,1920]{2,1,0:T(8,128)(2,1)S(1)} %fusion.7) | copy-start | bytes 2211844
  238.9 24.9 %collective-permute-start.17 = (bf16[48,1920]{1,0:T(8,128)(2,1)}, bf16[48,1920]{1,0:T(8,128)(2,1)}, u32[]{:S(2)}, u32[]{:S(2)}) collective-permute-start(bf16[48,1920]{1,0:T(8,128)(2,1)} %get-tuple-element.128), channel_id=1, source_target_pairs={{0,8},{2,10},{4,12},{6,14},{8,16},{10,18},{12,20},{14,22},{16,24},... | collective-permute-start | bytes 552968 | tf_op jit(solution)/shard_map/ppermute | solution.py:540
  242.4 21.4 %collective-permute-start.18 = (bf16[48,1920]{1,0:T(8,128)(2,1)}, bf16[48,1920]{1,0:T(8,128)(2,1)}, u32[]{:S(2)}, u32[]{:S(2)}) collective-permute-start(bf16[48,1920]{1,0:T(8,128)(2,1)} %get-tuple-element.130), channel_id=1, source_target_pairs={{0,16},{2,18},{4,20},{6,22},{8,24},{10,26},{12,28},{14,30},{16,0},... | collective-permute-start | bytes 552968 | tf_op jit(solution)/shard_map/ppermute | solution.py:540
  243.4 20.4 %collective-permute-start.19 = (bf16[48,1920]{1,0:T(8,128)(2,1)}, bf16[48,1920]{1,0:T(8,128)(2,1)}, u32[]{:S(2)}, u32[]{:S(2)}) collective-permute-start(bf16[48,1920]{1,0:T(8,128)(2,1)} %get-tuple-element.129), channel_id=1, source_target_pairs={{0,24},{2,26},{4,28},{6,30},{8,0},{10,2},{12,4},{14,6},{16,8},{18,... | collective-permute-start | bytes 552968 | tf_op jit(solution)/shard_map/ppermute | solution.py:540
  244.8 11.5 %collective-permute-start.20 = (f32[8,2048]{1,0:T(8,128)S(1)}, f32[8,2048]{1,0:T(8,128)S(1)}, u32[]{:S(2)}, u32[]{:S(2)}) collective-permute-start(f32[8,2048]{1,0:T(8,128)S(1)} %add.264), channel_id=1, source_target_pairs={{0,8},{2,10},{4,12},{6,14},{8,0},{10,2},{12,4},{14,6},{16,24},{18,... | collective-permute-start | bytes 196616 | tf_op jit(solution)/shard_map/ppermute | solution.py:536
  256.3 2.6 copy-start.8
  256.3 5.3 %collective-permute-start.21 = (f32[8,2048]{1,0:T(8,128)S(1)}, f32[8,2048]{1,0:T(8,128)}, u32[]{:S(2)}, u32[]{:S(2)}) collective-permute-start(f32[8,2048]{1,0:T(8,128)S(1)} %add.278), channel_id=1, source_target_pairs={{0,16},{2,18},{4,20},{6,22},{8,24},{10,26},{12,28},{14,30},{16,0},... | collective-permute-start | bytes 196616 | tf_op jit(solution)/shard_map/ppermute | solution.py:536
  257.0 1.9 copy-start.7
  257.0 4.7 %copy-start.18 = (f32[16,768]{1,0:T(8,128)S(1)}, f32[16,768]{1,0:T(8,128)}, u32[]{:S(2)}) copy-start(f32[16,768]{1,0:T(8,128)} %get-tuple-element.94) | copy-start | bytes 147460
  258.9 16.5 %copy-start.14 = (bf16[96]{0:T(256)(128)(2,1)S(1)}, bf16[96]{0:T(256)(128)(2,1)}, u32[]{:S(2)}) copy-start(bf16[96]{0:T(256)(128)(2,1)} %param.22) | copy-start | bytes 580
  258.9 8.2 %collective-permute-start.23 = (bf16[48,3072]{1,0:T(8,128)(2,1)S(1)}, bf16[48,3072]{1,0:T(8,128)(2,1)S(1)}, u32[]{:S(2)}, u32[]{:S(2)}) collective-permute-start(bf16[48,3072]{1,0:T(8,128)(2,1)S(1)} %copy-done.7), channel_id=1, source_target_pairs={{0,1},{1,0},{2,3},{3,2},{4,5},{5,4},{6,7},{7,6},{8,9},{9,8},{10,11... | collective-permute-start | bytes 884744 | tf_op jit(solution)/shard_map/ppermute | solution.py:536
  261.7 6.1 %collective-permute-start.22 = (f32[16,768]{1,0:T(8,128)S(1)}, f32[16,768]{1,0:T(8,128)S(1)}, u32[]{:S(2)}, u32[]{:S(2)}) collective-permute-start(f32[16,768]{1,0:T(8,128)S(1)} %copy-done.18), channel_id=1, source_target_pairs={{1,0},{3,2},{5,4},{7,6},{9,8},{11,10},{13,12},{15,14},{17,16},{19,... | collective-permute-start | bytes 147464 | tf_op jit(solution)/shard_map/ppermute | solution.py:867
  267.3 16.1 %copy-start.11 = (bf16[48]{0:T(256)(128)(2,1)S(1)}, bf16[48]{0:T(256)(128)(2,1)}, u32[]{:S(2)}) copy-start(bf16[48]{0:T(256)(128)(2,1)} %param.14) | copy-start | bytes 292
  267.7 2.9 %copy-start.9 = (f32[16,768]{1,0:T(8,128)}, f32[16,768]{1,0:T(8,128)S(1)}, u32[]{:S(2)}) copy-start(f32[16,768]{1,0:T(8,128)S(1)} %collective-permute-done.22) | copy-start | bytes 147460
  267.7 8.4 %collective-permute-start.25 = (f32[8,2048]{1,0:T(8,128)S(1)}, f32[8,2048]{1,0:T(8,128)}, u32[]{:S(2)}, u32[]{:S(2)}) collective-permute-start(f32[8,2048]{1,0:T(8,128)S(1)} %add.279), channel_id=1, source_target_pairs={{0,1},{1,0},{2,3},{3,2},{4,5},{5,4},{6,7},{7,6},{8,9},{9,8},{10,11... | collective-permute-start | bytes 196616 | tf_op jit(solution)/shard_map/ppermute | solution.py:536
  268.6 10.1 %collective-permute-start.24 = (bf16[48,1920]{1,0:T(8,128)(2,1)}, bf16[48,1920]{1,0:T(8,128)(2,1)}, u32[]{:S(2)}, u32[]{:S(2)}) collective-permute-start(bf16[48,1920]{1,0:T(8,128)(2,1)} %fusion.13), channel_id=1, source_target_pairs={{0,1},{1,0},{2,3},{3,2},{4,5},{5,4},{6,7},{7,6},{8,9},{9,8},{10,11... | collective-permute-start | bytes 552968 | tf_op jit(solution)/shard_map/ppermute | solution.py:536
  273.5 7.1 %copy-start.6 = (f32[2,48,768]{2,1,0:T(8,128)}, f32[2,48,768]{2,1,0:T(8,128)S(1)}, u32[]{:S(2)}) copy-start(f32[2,48,768]{2,1,0:T(8,128)S(1)} %copy.42) | copy-start | bytes 884740
  275.5 8.4 %copy-start = (f32[1,1024,768]{2,1,0:T(8,128)}, f32[1,1024,768]{2,1,0:T(8,128)S(1)}, u32[]{:S(2)}) copy-start(f32[1,1024,768]{2,1,0:T(8,128)S(1)} %bitcast_dynamic-update-slice_fusion.7) | copy-start | bytes 9437188
  (2 other events, 1.4 us)
Sparse Core Ops, SparseCore 0:
  26.4 58.4 all-gather.1
  141.0 75.9 reduce-scatter.1
where the time goes:
time: 292 us; the launch traced here: 291 us
  Pallas kernels  123 us (42%)
  waiting for transfers between devices  45.5 us (16%)
  starting transfers between devices  35 us (12%)
  other arithmetic  26.5 us (9%)
  local copies, waits for them, and re-layouts  23.6 us (8%)
  matrix products  22 us (8%)
  between operations  14.8 us (5%)
    pallas_call x1, Pallas kernels, shards(): pl.pallas_call(functools.partial(scan_back_kernel, width), grid=(nc + 1,)...  44.7 us
    pallas_call x1, Pallas kernels, shards(): pl.pallas_call(functools.partial(gate_kernel, n), grid=(nw,), in_specs=[p...  27.3 us
    pallas_call x1, Pallas kernels, shards(): pl.pallas_call(functools.partial(project_kernel, n), grid=(nw + 1,), in_s...  22.7 us
    ppermute x13, waiting for transfers between devices, flip(): return lax.ppermute(v, axis, [(s, s ^ bit) for s in range(n)])  19.2 us
    ppermute x9, starting transfers between devices, shift(): return lax.ppermute(v, axis, [(s, (s + by) % n) for s in range(n)])  16.9 us
    dot_general x3, matrix products, dot_tn(): lax.dot_general(a, b, (((0,), (0,)), ((), ())), preferred_element_type=F32)  14.8 us
    pallas_call x1, Pallas kernels, shards(): pl.pallas_call(stream_back_kernel, grid=(nc + 1,), in_specs=[pl.BlockSpec...  14.8 us
    ppermute x9, waiting for transfers between devices, shift(): return lax.ppermute(v, axis, [(s, (s + by) % n) for s in range(n)])  14.5 us
  transfers between devices with their start and end apart: 28, of which 10 were waited for; matrix products, arithmetic and copies ran while one was open for 16% of the time, Pallas kernels for 33%

commit v1 on v0

--- a/solution.py
+++ b/solution.py
@@ -17,13 +17,10 @@
 HALO = 16
 BF = jnp.bfloat16
 F32 = jnp.float32
-EXACT = lax.Precision.HIGHEST
-
-
-def dot(a, b, precision=None):
-    return lax.dot_general(
-        a, b, (((1,), (0,)), ((), ())), precision=precision, preferred_element_type=F32
-    )
+
+
+def dot(a, b):
+    return lax.dot_general(a, b, (((1,), (0,)), ((), ())), preferred_element_type=F32)
 
 
 def dot_nt(a, b):
@@ -52,6 +49,12 @@
     hi = v.astype(BF).astype(F32)
     mid = (v - hi).astype(BF).astype(F32)
     return hi, mid, (v - hi - mid).astype(BF).astype(F32)
+
+
+def choose_sum(chosen, v):
+    w = v.shape[1]
+    got = dot(chosen.astype(BF), jnp.concatenate(three_terms(v), axis=1).astype(BF))
+    return got[:, :w] + got[:, w : 2 * w] + got[:, 2 * w :]
 
 
 def gap_left(cum, sign):
@@ -153,7 +156,7 @@
         weights, ends = [], []
         for p in range(WIDE // Q):
             part = slice(Q * p, Q * (p + 1))
-            cum = dot(lower, hp_ref[1:2, :] * step[part], EXACT)
+            cum = choose_sum(lower, hp_ref[1:2, :] * step[part])
             cum_ref[part, :] = cum
             last = cum[Q - 1 : Q, :]
             base_ref[8 * p : 8 * (p + 1), :] = base[...]
@@ -468,11 +471,8 @@
         upper = causal.astype(F32)
         strict = tri(Q, Q, lambda r, c: c < r).astype(F32)
         row_sums = row_sums[0:8] + row_sums[8:16]
-        d_decay = (
-            dot(upper, kcol[...].T + sums[:Q] - krow, EXACT)
-            + dot(strict, sums[Q : 2 * Q], EXACT)
-            + at_end * row_sums[0:1]
-        )
+        pairs = jnp.concatenate([kcol[...].T + sums[:Q] - krow, sums[Q : 2 * Q]], axis=0)
+        d_decay = choose_sum(jnp.concatenate([upper, strict], axis=1), pairs) + at_end * row_sums[0:1]
         d_dt = (sums[2 * Q :] + nega * d_decay) * sigmoid(dtv)
         d_ref[:, cd:] = d_dt.astype(BF)
         ghead_ref[0:1, :] += jnp.sum(d_dt, axis=0, keepdims=True)
@@ -789,7 +789,8 @@
     gin = carry(gst, -1)
     g_z = dot_tn(nrm[WIDE:], dz).astype(BF)
     g_out = dot_tn(mixed, cot.astype(BF)).astype(BF)
-    g_zo = jnp.concatenate([g_z, g_out.reshape(n, per, rows, d).transpose(0, 2, 1, 3).reshape(d, di)], axis=1)
+    g_zo = [g_z[:, d * k : d * (k + 1)].reshape(n, rows, d) for k in range(per)] + [g_out.reshape(n, rows * per, d)]
+    g_zo = jnp.concatenate(g_zo, axis=1).reshape(2 * di, d)
     g_zo = lax.psum_scatter(g_zo, "seq", scatter_dimension=0, tiled=True)
     args = (xc, slope, dtv, cum, start, gin, dsc, cin, cin, small, head_rows, skip, ee, er, hot, pick, behind)
 
@@ -830,14 +831,15 @@
 
     packed = jnp.concatenate([gconv, jnp.pad(ghead, ((0, 0), (0, LANES)))], axis=1)
     steps = sum_steps(n, hx)
+    packed = steps[0](packed)
     g_x = dot_tn(nrm[WIDE - Q :], dx).astype(BF)
     g_x, dz, packed = together(g_x, dz, packed)
     g_x = pair_scatter(g_x.reshape(n // 4, 2, 2, rows, cdp), n, 1, 2)
-    packed = steps[0](packed)
+    packed = steps[1](packed)
     dnz = dot_nt(dz, wzo[:, :di])
     g_x, packed, dnz, dx = together(g_x, packed, dnz, dx)
     g_x = pair_scatter(g_x, n, 2, 1)
-    packed = steps[1](packed)
+    packed = steps[2](packed)
 
     args = (dx, dnz, wa, wb, small, s, halo, cot)
     g_stream, msg = pl.pallas_call(
@@ -861,16 +863,16 @@
     )(*args)
     g_x, packed, msg, g_zo = together(g_x, packed, msg, g_zo)
     g_zo = over_hx(g_zo, hx)
+    msg = lax.ppermute(msg, "hx", [(r + 1, r) for r in range(hx - 1)])
     g_x = far_scatter(g_x, n)
-    for step in steps[2:-1]:
+    for step in steps[3:-1]:
         packed = step(packed)
-    msg = lax.ppermute(msg, "hx", [(r + 1, r) for r in range(hx - 1)])
-    g_x, packed, msg, g_zo = together(g_x, packed, msg, g_zo)
     g_x = over_hx(g_x, hx)
     packed = steps[-1](packed)
     g_stream = lax.dynamic_update_slice(g_stream, g_stream[t - HALO :] + msg, (t - HALO, 0))
     mine = lax.dynamic_slice_in_dim(packed[:, :cd], lax.axis_index("seq") * (cd // n), cd // n, 1)
-    g_z, g_out = g_zo[:, :di], g_zo[:, di:].reshape(rows, per, d).transpose(1, 0, 2).reshape(rows * per, d)
+    g_z = jnp.concatenate([g_zo[rows * k : rows * (k + 1)] for k in range(per)], axis=1)
+    g_out = g_zo[rows * per :]
     g_main = jnp.concatenate([g_z, g_x[:, :cd]], axis=1)
     g_dt = g_x[:, cd : cd + heads]
     g_norm = (

time: 292 us -> 277 us (0.949)
  waiting for transfers between devices: 45.5 us -> 41 us
  local copies, waits for them, and re-layouts: 23.6 us -> 19.3 us
  other arithmetic: 26.5 us -> 22.9 us
    ppermute x13, waiting for transfers between devices: 19.2 us -> 14.4 us  [flip(): return lax.ppermute(v, axis, [(s, s ^ bit) for s in range(n)])]
    reshape x2 -> x0, local copies, waits for them, and re-layouts: 4.06 us -> none  [the longest x1 2.19 us: shards(): g_out.reshape(n, per, rows, d).transpose(0, 2, 1, 3).reshape(d, di)]
    ppermute x9, starting transfers between devices: 16.9 us -> 13.4 us  [shift(): return lax.ppermute(v, axis, [(s, (s + by) % n) for s in range(n)])]
    unnamed x49 -> x44, local copies, waits for them, and re-layouts: 8.63 us -> 11.7 us
  transfers between devices with their start and end apart: 28 -> 28, of which waited for: 10 -> 9; matrix products, arithmetic and copies ran while one was open for 16% -> 16% of each run, Pallas kernels for 33% -> 35%
where the time goes in v1:
time: 277 us; the launch traced here: 276 us
  Pallas kernels  123 us (44%)
  waiting for transfers between devices  41 us (15%)
  starting transfers between devices  33.5 us (12%)
  other arithmetic  22.9 us (8%)
  matrix products  21.8 us (8%)
  local copies, waits for them, and re-layouts  19.3 us (7%)
  between operations  14.8 us (5%)
    pallas_call x1, Pallas kernels, shards(): pl.pallas_call(functools.partial(scan_back_kernel, width), grid=(nc + 1,)...  44.3 us
    pallas_call x1, Pallas kernels, shards(): pl.pallas_call(functools.partial(gate_kernel, n), grid=(nw,), in_specs=[p...  27.3 us
    pallas_call x1, Pallas kernels, shards(): pl.pallas_call(functools.partial(project_kernel, n), grid=(nw + 1,), in_s...  22.4 us
    ppermute x9, waiting for transfers between devices, shift(): return lax.ppermute(v, axis, [(s, (s + by) % n) for s in range(n)])  15.3 us
    dot_general x3, matrix products, dot_tn(): lax.dot_general(a, b, (((0,), (0,)), ((), ())), preferred_element_type=F32)  14.8 us
    pallas_call x1, Pallas kernels, shards(): pl.pallas_call(stream_back_kernel, grid=(nc + 1,), in_specs=[pl.BlockSpec...  14.8 us
    ppermute x13, waiting for transfers between devices, flip(): return lax.ppermute(v, axis, [(s, s ^ bit) for s in range(n)])  14.4 us
    pallas_call x1, Pallas kernels, shards(): pl.pallas_call(functools.partial(intra_kernel, width), grid=(nc,), in_spe...  13.8 us
  transfers between devices with their start and end apart: 28, of which 9 were waited for; matrix products, arithmetic and copies ran while one was open for 16% of the time, Pallas kernels for 35%

profile of v1, /device:TPU:0, one launch (start us, length us, event | category | flops | bytes accessed | tf_op | source)
XLA Modules:
  0.0 276.0 jit_solution(285610639894461600)
XLA Ops:
  7.3 0.9 slice.72
  8.2 3.1 %collective-permute-start.1 = (bf16[48,1280]{1,0:T(8,128)(2,1)S(1)}, bf16[48,1280]{1,0:T(8,128)(2,1)S(1)}, u32[]{:S(2)}, u32[]{:S(2)}) collective-permute-start(bf16[48,1280]{1,0:T(8,128)(2,1)S(1)} %slice.72), channel_id=1, source_target_pairs={{0,8},{2,10},{4,12},{6,14},{8,16},{10,18},{12,20},{14,22},{16,24},... | collective-permute-start | bytes 368648 | tf_op jit(solution)/shard_map/ppermute | solution.py:540
  11.3 2.6 collective-permute-start.2
  13.9 1.3 collective-permute-start.3
  15.2 0.9 slice.73
  17.7 1.6 collective-permute-start.6
  20.1 3.4 %collective-permute-start = (f32[16,768]{1,0:T(8,128)S(1)}, f32[16,768]{1,0:T(8,128)S(1)}, u32[]{:S(2)}, u32[]{:S(2)}) collective-permute-start(f32[16,768]{1,0:T(8,128)S(1)} %slice_bitcast_fusion), channel_id=1, source_target_pairs={{0,1},{2,3},{4,5},{6,7},{8,9},{10,11},{12,13},{14,15},{16,17},{18,... | collective-permute-start | bytes 147464 | tf_op jit(solution)/shard_map/ppermute | solution.py:645
  23.5 0.9 slice.75
  24.4 1.0 copy.37
  28.9 1.0 add_convert_fusion.ee_ref
  30.0 1.0 fusion.8.er_ref
  31.0 2.1 fusion.6.hot_ref
  33.1 1.2 and_convert_fusion.pick_ref
  36.2 2.9 %collective-permute-start.9 = (bf16[2,48,768]{2,1,0:T(8,128)(2,1)S(1)}, bf16[2,48,768]{2,1,0:T(8,128)(2,1)S(1)}, u32[]{:S(2)}, u32[]{:S(2)}) collective-permute-start(bf16[2,48,768]{2,1,0:T(8,128)(2,1)S(1)} %maximum_select_fusion.4), channel_id=1, source_target_pairs={{0,24},{2,26},{4,28},{6,30},{8,0},{10,2},{12,4},{14,6},{16,8},{18,... | collective-permute-start | bytes 442376 | tf_op jit(solution)/shard_map/ppermute | solution.py:540
  39.7 6.7 %collective-permute-done.7 = bf16[2,48,768]{2,1,0:T(8,128)(2,1)S(1)} collective-permute-done((bf16[2,48,768]{2,1,0:T(8,128)(2,1)S(1)}, bf16[2,48,768]{2,1,0:T(8,128)(2,1)S(1)}, u32[]{:S(2)}, u32[]{:S(2)}) %collective-permute-start.7) | collective-permute-done | bytes 147488 | tf_op jit(solution)/shard_map/ppermute | solution.py:540
  46.4 7.8 %collective-permute-done.8 = bf16[2,48,768]{2,1,0:T(8,128)(2,1)S(1)} collective-permute-done((bf16[2,48,768]{2,1,0:T(8,128)(2,1)S(1)}, bf16[2,48,768]{2,1,0:T(8,128)(2,1)S(1)}, u32[]{:S(2)}, u32[]{:S(2)}) %collective-permute-start.8) | collective-permute-done | bytes 147488 | tf_op jit(solution)/shard_map/ppermute | solution.py:540
  55.3 1.0 collective-permute-done.10
  56.3 1.1 maximum_select_fusion.1
  57.7 1.5 maximum_select_fusion
  59.9 22.4 %project.1 = (bf16[1280,768]{1,0:T(8,128)(2,1)}, bf16[1280,1792]{1,0:T(8,128)(2,1)}, bf16[1024,1792]{1,0:T(8,128)(2,1)}, bf16[1024,1792]{1,0:T(8,128)(2,1)}, f32...) custom-call(f32[16,768]{1,0:T(8,128)} %copy-done.6, ...), custom_call_target="tpu_custom_call" | custom-call | flops 4529848320 | bytes 12582912 | tf_op jit(solution)/shard_map/project/pallas_call | solution.py:672
  82.3 3.0 %collective-permute-start.11 = (bf16[128,1536]{1,0:T(8,128)(2,1)}, bf16[128,1536]{1,0:T(8,128)(2,1)S(1)}, u32[]{:S(2)}, u32[]{:S(2)}) collective-permute-start(bf16[128,1536]{1,0:T(8,128)(2,1)} %get-tuple-element.63), channel_id=1, source_target_pairs={{0,1},{2,3},{4,5},{6,7},{8,9},{10,11},{12,13},{14,15},{16,17},{18,... | collective-permute-start | bytes 1179656 | tf_op jit(solution)/shard_map/ppermute | solution.py:710
  85.3 13.8 %intra.1.yi_ref = bf16[1024,1536]{1,0:T(8,128)(2,1)} custom-call(bf16[1024,1792]{1,0:T(8,128)(2,1)} %get-tuple-element.55.xc_ref.c_ref, f32[1024,128]{1,0:T(8,128)} %get-tuple-element.56.dtv_ref, f32[1024,128]{1,0:T(8,128)} %get-tuple-element.57.cum_ref, f32[1,1536]{1,0:T(1,128)} %broadcast_in_dim_reshape.3.skip_ref, ...), custom_call_target="tpu_custom_call" | custom-call | flops 2415919104 | bytes 7340032 | tf_op jit(solution)/shard_map/intra/pallas_call | solution.py:724
  99.9 27.3 %gate.1 = (f32[1024,768]{1,0:T(8,128)}, bf16[1024,1536]{1,0:T(8,128)(2,1)}, bf16[1024,1536]{1,0:T(8,128)(2,1)}, bf16[1024,1536]{1,0:T(8,128)(2,1)}, bf16[8,128,1...) custom-call(bf16[1024,1536]{1,0:T(8,128)(2,1)} %intra.1.yi_ref, bf16[1280,768]{1,0:T(8,128)(2,1)} %get-tuple-element.60.nrm_ref, ...), custom_call_target="tpu_custom_call" | custom-call | flops 7247757312 | bytes 22544384 | tf_op jit(solution)/shard_map/gate/pallas_call | solution.py:744
  127.2 4.9 %convolution_convert_fusion.1 = bf16[768,1536]{1,0:T(8,128)(2,1)S(1)} fusion(bf16[1024,1536]{1,0:T(8,128)(2,1)} %get-tuple-element.80, bf16[1280,768]{1,0:T(8,128)(2,1)S(1)} %copy-done.18), kind=kOutput, calls=%fused_computation.2 | convolution fusion | flops 2417098752 | bytes 7077888 | tf_op jit(solution)/shard_map/dot_general | solution.py:31
  132.4 1.7 copy-done
  134.1 3.0 %fusion.53 = bf16[1536,768]{1,0:T(8,128)(2,1)S(1)} fusion(bf16[1024,1536]{1,0:T(8,128)(2,1)S(1)} %copy-done.17, f32[1,1024,768]{2,1,0:T(8,128)S(1)} %copy-done), kind=kOutput, calls=%fused_computation.129 | convolution fusion | flops 2415919104 | bytes 8650752 | tf_op jit(solution)/shard_map/dot_general | solution.py:31
  137.0 2.4 pad_maximum_fusion
  139.4 1.0 copy-done.12
  140.4 1.5 collective-permute-start.12
  141.9 11.3 %collective-permute-done.12.gin_ref = bf16[128,1536]{1,0:T(8,128)(2,1)S(1)} collective-permute-done((bf16[128,1536]{1,0:T(8,128)(2,1)S(1)}, bf16[128,1536]{1,0:T(8,128)(2,1)S(1)}, u32[]{:S(2)}, u32[]{:S(2)}) %collective-permute-start.12) | collective-permute-done | bytes 393248 | tf_op jit(solution)/shard_map/ppermute | solution.py:710
  153.9 44.3 %scan_back.1 = (bf16[1152,1920]{1,0:T(8,128)(2,1)}, f32[8,1792]{1,0:T(8,128)}, f32[8,128]{1,0:T(8,128)}) custom-call(bf16[1024,1792]{1,0:T(8,128)(2,1)} %get-tuple-element.55.xc_ref.c_ref, bf16[1024,1792]{1,0:T(8,128)(2,1)} %get-tuple-element.66.slope_ref, f32[1024,128]{1,0:T(8,128)} %get-tuple-element.56.dtv_ref, f32[1024,128]{1,0:T(8,128)} %get-tuple-element.57.cum_ref, ...), custom_call_target="tpu_custom_call" | custom-call | flops 9663676416 | bytes 14680064 | tf_op jit(solution)/shard_map/scan_back/pallas_call | solution.py:800
  199.1 6.9 %convolution_convert_fusion.2 = bf16[768,1920]{1,0:T(8,128)(2,1)S(1)} fusion(bf16[1152,1920]{1,0:T(8,128)(2,1)} %get-tuple-element.81.d_ref, bf16[1280,768]{1,0:T(8,128)(2,1)S(1)} %copy-done.19), kind=kOutput, calls=%fused_computation.3 | convolution fusion | flops 3398860800 | bytes 9142272 | tf_op jit(solution)/shard_map/dot_general | solution.py:31
  206.1 1.6 copy-done.1
  208.3 1.2 collective-permute-start.15
  209.5 7.0 %fusion.1.dnz_ref = f32[1024,768]{1,0:T(8,128)} fusion(bf16[1024,1536]{1,0:T(8,128)(2,1)} %get-tuple-element.80, bf16[768,3072]{1,0:T(8,128)(2,1)} %all-gather.2.cloned.1.call-done.wzo_ref), kind=kOutput, calls=%fused_computation.6 | convolution fusion | flops 2415919104 | bytes 8650752 | tf_op jit(solution)/shard_map/dot_general | solution.py:27
  216.5 1.8 fusion
  218.4 1.0 collective-permute-start.16
  219.4 3.7 %collective-permute-start.17 = (f32[8,2048]{1,0:T(8,128)S(1)}, f32[8,2048]{1,0:T(8,128)S(1)}, u32[]{:S(2)}, u32[]{:S(2)}) collective-permute-start(f32[8,2048]{1,0:T(8,128)S(1)} %add.261), channel_id=1, source_target_pairs={{0,8},{2,10},{4,12},{6,14},{8,0},{10,2},{12,4},{14,6},{16,24},{18,... | collective-permute-start | bytes 196616 | tf_op jit(solution)/shard_map/ppermute | solution.py:536
  223.1 14.8 %stream_back.1 = (f32[1024,768]{1,0:T(8,128)}, f32[16,768]{1,0:T(8,128)}) custom-call(bf16[1152,1920]{1,0:T(8,128)(2,1)} %get-tuple-element.81.d_ref, f32[1024,768]{1,0:T(8,128)} %fusion.1.dnz_ref, bf16[768,1280]{1,0:T(8,128)(2,1)} %bitcast.98, bf16[768,768]{1,0:T(8,128)(2,1)} %bitcast.102, f32[8,1792]{1,0:T(8,128)} %get-tuple-element.64.small_ref, ...), custom_call_target="tpu_custom_call" | custom-call | flops 3019898880 | bytes 15728640 | tf_op jit(solution)/shard_map/stream_back/pallas_call | solution.py:845
  237.8 3.8 %copy.54 = f32[1,1024,768]{2,1,0:T(8,128)} copy(f32[1,1024,768]{2,1,0:T(8,128)} %bitcast.105) | data formatting | bytes 6291456
  242.7 1.3 collective-permute-start.18
  244.6 1.8 collective-permute-start.21
  246.4 7.8 %collective-permute-done.24 = f32[8,2048]{1,0:T(8,128)S(1)} collective-permute-done((f32[8,2048]{1,0:T(8,128)S(1)}, f32[8,2048]{1,0:T(8,128)S(1)}, u32[]{:S(2)}, u32[]{:S(2)}) %collective-permute-start.24) | collective-permute-done | bytes 65568 | tf_op jit(solution)/shard_map/ppermute | solution.py:536
  254.3 1.4 bitcast_dynamic-update-slice_fusion.7
  255.7 2.8 %collective-permute-done.25 = f32[8,2048]{1,0:T(8,128)S(1)} collective-permute-done((f32[8,2048]{1,0:T(8,128)S(1)}, f32[8,2048]{1,0:T(8,128)S(1)}, u32[]{:S(2)}, u32[]{:S(2)}) %collective-permute-start.25) | collective-permute-done | bytes 65568 | tf_op jit(solution)/shard_map/ppermute | solution.py:536
  262.0 1.0 convert_add_fusion.2
  264.5 2.4 collective-permute-done.23
  267.7 1.0 multiply_reduce_fusion
  (132 shorter events, 21.3 us)
Async XLA Ops:
  7.2 22.8 %copy-start.3 = (bf16[48,3328]{1,0:T(8,128)(2,1)S(1)}, bf16[48,3328]{1,0:T(8,128)(2,1)}, u32[]{:S(2)}) copy-start(bf16[48,3328]{1,0:T(8,128)(2,1)} %param.15) | copy-start | bytes 958468
  7.2 19.3 %copy-start.9 = (f32[24]{0:T(128)S(1)}, f32[24]{0:T(128)}, u32[]{:S(2)}) copy-start(f32[24]{0:T(128)} %param.21) | copy-start | bytes 292
  7.2 20.0 %copy-start.16 = (f32[24]{0:T(128)S(1)}, f32[24]{0:T(128)}, u32[]{:S(2)}) copy-start(f32[24]{0:T(128)} %param.20) | copy-start | bytes 292
  7.2 91.9 %all-gather.2.cloned.1.call-start = ((), (), s32[]{:S(2)}) async-start(), calls=%async_computation.1 | async-start | bytes 5013504 | tf_op jit(solution)/shard_map/all_gather | solution.py:644
  8.2 27.5 %collective-permute-start.1 = (bf16[48,1280]{1,0:T(8,128)(2,1)S(1)}, bf16[48,1280]{1,0:T(8,128)(2,1)S(1)}, u32[]{:S(2)}, u32[]{:S(2)}) collective-permute-start(bf16[48,1280]{1,0:T(8,128)(2,1)S(1)} %slice.72), channel_id=1, source_target_pairs={{0,8},{2,10},{4,12},{6,14},{8,16},{10,18},{12,20},{14,22},{16,24},... | collective-permute-start | bytes 368648 | tf_op jit(solution)/shard_map/ppermute | solution.py:540
  11.3 24.9 %collective-permute-start.2 = (bf16[48,1280]{1,0:T(8,128)(2,1)S(1)}, bf16[48,1280]{1,0:T(8,128)(2,1)S(1)}, u32[]{:S(2)}, u32[]{:S(2)}) collective-permute-start(bf16[48,1280]{1,0:T(8,128)(2,1)S(1)} %slice.72), channel_id=1, source_target_pairs={{0,16},{2,18},{4,20},{6,22},{8,24},{10,26},{12,28},{14,30},{16,0},... | collective-permute-start | bytes 368648 | tf_op jit(solution)/shard_map/ppermute | solution.py:540
  13.9 25.2 %collective-permute-start.3 = (bf16[48,1280]{1,0:T(8,128)(2,1)S(1)}, bf16[48,1280]{1,0:T(8,128)(2,1)S(1)}, u32[]{:S(2)}, u32[]{:S(2)}) collective-permute-start(bf16[48,1280]{1,0:T(8,128)(2,1)S(1)} %slice.72), channel_id=1, source_target_pairs={{0,24},{2,26},{4,28},{6,30},{8,0},{10,2},{12,4},{14,6},{16,8},{18,... | collective-permute-start | bytes 368648 | tf_op jit(solution)/shard_map/ppermute | solution.py:540
  17.7 17.2 %collective-permute-start.6 = (bf16[48,768]{1,0:T(8,128)(2,1)S(1)}, bf16[48,768]{1,0:T(8,128)(2,1)S(1)}, u32[]{:S(2)}, u32[]{:S(2)}) collective-permute-start(bf16[48,768]{1,0:T(8,128)(2,1)S(1)} %fusion.21), channel_id=1, source_target_pairs={{0,4},{2,6},{4,0},{6,2},{8,12},{10,14},{12,8},{14,10},{16,20},{18,... | collective-permute-start | bytes 221192 | tf_op jit(solution)/shard_map/ppermute | solution.py:536
  20.1 39.2 %collective-permute-start = (f32[16,768]{1,0:T(8,128)S(1)}, f32[16,768]{1,0:T(8,128)S(1)}, u32[]{:S(2)}, u32[]{:S(2)}) collective-permute-start(f32[16,768]{1,0:T(8,128)S(1)} %slice_bitcast_fusion), channel_id=1, source_target_pairs={{0,1},{2,3},{4,5},{6,7},{8,9},{10,11},{12,13},{14,15},{16,17},{18,... | collective-permute-start | bytes 147464 | tf_op jit(solution)/shard_map/ppermute | solution.py:645
  25.4 8.9 %copy-start.10 = (f32[24]{0:T(128)S(1)}, f32[24]{0:T(128)}, u32[]{:S(2)}) copy-start(f32[24]{0:T(128)} %param.19) | copy-start | bytes 292
  26.2 215.6 %reduce-scatter.2.cloned.1.call-start = ((), (), s32[]{:S(2)}) async-start(), calls=%async_computation.2 | async-start | bytes 5013504 | tf_op jit(solution)/shard_map/reduce_scatter | solution.py:794
  34.9 11.5 %collective-permute-start.7 = (bf16[2,48,768]{2,1,0:T(8,128)(2,1)S(1)}, bf16[2,48,768]{2,1,0:T(8,128)(2,1)S(1)}, u32[]{:S(2)}, u32[]{:S(2)}) collective-permute-start(bf16[2,48,768]{2,1,0:T(8,128)(2,1)S(1)} %maximum_select_fusion.4), channel_id=1, source_target_pairs={{0,8},{2,10},{4,12},{6,14},{8,16},{10,18},{12,20},{14,22},{16,24},... | collective-permute-start | bytes 442376 | tf_op jit(solution)/shard_map/ppermute | solution.py:540
  35.7 18.5 %collective-permute-start.8 = (bf16[2,48,768]{2,1,0:T(8,128)(2,1)S(1)}, bf16[2,48,768]{2,1,0:T(8,128)(2,1)S(1)}, u32[]{:S(2)}, u32[]{:S(2)}) collective-permute-start(bf16[2,48,768]{2,1,0:T(8,128)(2,1)S(1)} %maximum_select_fusion.4), channel_id=1, source_target_pairs={{0,16},{2,18},{4,20},{6,22},{8,24},{10,26},{12,28},{14,30},{16,0},... | collective-permute-start | bytes 442376 | tf_op jit(solution)/shard_map/ppermute | solution.py:540
  36.2 18.1 %collective-permute-start.9 = (bf16[2,48,768]{2,1,0:T(8,128)(2,1)S(1)}, bf16[2,48,768]{2,1,0:T(8,128)(2,1)S(1)}, u32[]{:S(2)}, u32[]{:S(2)}) collective-permute-start(bf16[2,48,768]{2,1,0:T(8,128)(2,1)S(1)} %maximum_select_fusion.4), channel_id=1, source_target_pairs={{0,24},{2,26},{4,28},{6,30},{8,0},{10,2},{12,4},{14,6},{16,8},{18,... | collective-permute-start | bytes 442376 | tf_op jit(solution)/shard_map/ppermute | solution.py:540
  39.1 15.2 %collective-permute-start.4 = (bf16[4,48,1280]{2,1,0:T(8,128)(2,1)S(1)}, bf16[4,48,1280]{2,1,0:T(8,128)(2,1)S(1)}, u32[]{:S(2)}, u32[]{:S(2)}) collective-permute-start(bf16[4,48,1280]{2,1,0:T(8,128)(2,1)S(1)} %bitcast_dynamic-update-slice_fusion.3), channel_id=1, source_target_pairs={{0,4},{2,6},{4,0},{6,2},{8,12},{10,14},{12,8},{14,10},{16,20},{18,... | collective-permute-start | bytes 1474568 | tf_op jit(solution)/shard_map/ppermute | solution.py:536
  54.3 2.1 collective-permute-start.10
  54.4 3.3 %collective-permute-start.5 = (bf16[4,2,48,1280]{3,2,1,0:T(8,128)(2,1)S(1)}, bf16[4,2,48,1280]{3,2,1,0:T(8,128)(2,1)S(1)}, u32[]{:S(2)}, u32[]{:S(2)}) collective-permute-start(bf16[4,2,48,1280]{3,2,1,0:T(8,128)(2,1)S(1)} %maximum_select_fusion.2), channel_id=1, source_target_pairs={{0,2},{2,0},{4,6},{6,4},{8,10},{10,8},{12,14},{14,12},{16,18},{18,... | collective-permute-start | bytes 2949128 | tf_op jit(solution)/shard_map/ppermute | solution.py:536
  59.3 0.6 copy-start.6
  82.3 16.8 %collective-permute-start.11 = (bf16[128,1536]{1,0:T(8,128)(2,1)}, bf16[128,1536]{1,0:T(8,128)(2,1)S(1)}, u32[]{:S(2)}, u32[]{:S(2)}) collective-permute-start(bf16[128,1536]{1,0:T(8,128)(2,1)} %get-tuple-element.63), channel_id=1, source_target_pairs={{0,1},{2,3},{4,5},{6,7},{8,9},{10,11},{12,13},{14,15},{16,17},{18,... | collective-permute-start | bytes 1179656 | tf_op jit(solution)/shard_map/ppermute | solution.py:710
  99.1 0.8 copy-start.14
  99.9 27.3 %copy-start.18 = (bf16[1280,768]{1,0:T(8,128)(2,1)S(1)}, bf16[1280,768]{1,0:T(8,128)(2,1)}, u32[]{:S(2)}) copy-start(bf16[1280,768]{1,0:T(8,128)(2,1)} %get-tuple-element.60.nrm_ref) | copy-start | bytes 5898244
  127.2 5.1 %copy-start.17 = (bf16[1024,1536]{1,0:T(8,128)(2,1)S(1)}, bf16[1024,1536]{1,0:T(8,128)(2,1)}, u32[]{:S(2)}) copy-start(bf16[1024,1536]{1,0:T(8,128)(2,1)} %get-tuple-element.87) | copy-start | bytes 9437188
  132.2 1.9 copy-start
  139.4 1.0 copy-start.12
  140.4 12.8 %collective-permute-start.12 = (bf16[128,1536]{1,0:T(8,128)(2,1)S(1)}, bf16[128,1536]{1,0:T(8,128)(2,1)S(1)}, u32[]{:S(2)}, u32[]{:S(2)}) collective-permute-start(bf16[128,1536]{1,0:T(8,128)(2,1)S(1)} %copy-done.12), channel_id=1, source_target_pairs={{1,0},{3,2},{5,4},{7,6},{9,8},{11,10},{13,12},{15,14},{17,16},{19,... | collective-permute-start | bytes 1179656 | tf_op jit(solution)/shard_map/ppermute | solution.py:710
  153.2 0.7 copy-start.13
  153.9 45.2 %copy-start.19 = (bf16[1280,768]{1,0:T(8,128)(2,1)S(1)}, bf16[1280,768]{1,0:T(8,128)(2,1)}, u32[]{:S(2)}) copy-start(bf16[1280,768]{1,0:T(8,128)(2,1)} %get-tuple-element.60.nrm_ref) | copy-start | bytes 5898244
  199.1 7.0 %collective-permute-start.13 = (f32[8,2048]{1,0:T(8,128)S(1)}, f32[8,2048]{1,0:T(8,128)S(1)}, u32[]{:S(2)}, u32[]{:S(2)}) collective-permute-start(f32[8,2048]{1,0:T(8,128)S(1)} %select_maximum_fusion), channel_id=1, source_target_pairs={{0,2},{2,0},{4,6},{6,4},{8,10},{10,8},{12,14},{14,12},{16,18},{18,... | collective-permute-start | bytes 196616 | tf_op jit(solution)/shard_map/ppermute | solution.py:536
  199.1 7.0 %copy-start.5 = (f32[8,1792]{1,0:T(8,128)S(1)}, f32[8,1792]{1,0:T(8,128)}, u32[]{:S(2)}) copy-start(f32[8,1792]{1,0:T(8,128)} %get-tuple-element.76) | copy-start | bytes 172036
  199.1 7.0 %copy-start.7 = (f32[8,128]{1,0:T(8,128)S(1)}, f32[8,128]{1,0:T(8,128)}, u32[]{:S(2)}) copy-start(f32[8,128]{1,0:T(8,128)} %get-tuple-element.77) | copy-start | bytes 12292
  206.1 1.6 copy-start.1
  207.8 8.7 %collective-permute-start.14 = (bf16[4,2,48,1920]{3,2,1,0:T(8,128)(2,1)S(1)}, bf16[4,2,48,1920]{3,2,1,0:T(8,128)(2,1)}, u32[]{:S(2)}, u32[]{:S(2)}) collective-permute-start(bf16[4,2,48,1920]{3,2,1,0:T(8,128)(2,1)S(1)} %dynamic-slice_bitcast_fusion), channel_id=1, source_target_pairs={{0,2},{2,0},{4,6},{6,4},{8,10},{10,8},{12,14},{14,12},{16,18},{18,... | collective-permute-start | bytes 4423688 | tf_op jit(solution)/shard_map/ppermute | solution.py:536
  208.3 8.2 %copy-start.2 = (bf16[768,1920]{1,0:T(8,128)(2,1)S(1)}, bf16[768,1920]{1,0:T(8,128)(2,1)}, u32[]{:S(2)}) copy-start(bf16[768,1920]{1,0:T(8,128)(2,1)} %copy-done.1) | copy-start | bytes 8847364
  208.3 8.2 %collective-permute-start.15 = (f32[8,2048]{1,0:T(8,128)S(1)}, f32[8,2048]{1,0:T(8,128)S(1)}, u32[]{:S(2)}, u32[]{:S(2)}) collective-permute-start(f32[8,2048]{1,0:T(8,128)S(1)} %fusion.48), channel_id=1, source_target_pairs={{0,4},{2,6},{4,0},{6,2},{8,12},{10,14},{12,8},{14,10},{16,20},{18,... | collective-permute-start | bytes 196616 | tf_op jit(solution)/shard_map/ppermute | solution.py:536
  218.4 23.2 %collective-permute-start.16 = (bf16[4,48,1920]{2,1,0:T(8,128)(2,1)S(1)}, bf16[4,48,1920]{2,1,0:T(8,128)(2,1)S(1)}, u32[]{:S(2)}, u32[]{:S(2)}) collective-permute-start(bf16[4,48,1920]{2,1,0:T(8,128)(2,1)S(1)} %dynamic-slice_bitcast_fusion.1), channel_id=1, source_target_pairs={{0,4},{2,6},{4,0},{6,2},{8,12},{10,14},{12,8},{14,10},{16,20},{18,... | collective-permute-start | bytes 2211848 | tf_op jit(solution)/shard_map/ppermute | solution.py:536
  219.4 22.2 %collective-permute-start.17 = (f32[8,2048]{1,0:T(8,128)S(1)}, f32[8,2048]{1,0:T(8,128)S(1)}, u32[]{:S(2)}, u32[]{:S(2)}) collective-permute-start(f32[8,2048]{1,0:T(8,128)S(1)} %add.261), channel_id=1, source_target_pairs={{0,8},{2,10},{4,12},{6,14},{8,0},{10,2},{12,4},{14,6},{16,24},{18,... | collective-permute-start | bytes 196616 | tf_op jit(solution)/shard_map/ppermute | solution.py:536
  237.8 4.9 %copy-start.15 = (f32[16,768]{1,0:T(8,128)S(1)}, f32[16,768]{1,0:T(8,128)}, u32[]{:S(2)}) copy-start(f32[16,768]{1,0:T(8,128)} %get-tuple-element.88) | copy-start | bytes 147460
  241.6 21.5 %copy-start.4 = (bf16[96,768]{1,0:T(8,128)(2,1)S(1)}, bf16[96,768]{1,0:T(8,128)(2,1)}, u32[]{:S(2)}) copy-start(bf16[96,768]{1,0:T(8,128)(2,1)} %param.23) | copy-start | bytes 442372
  241.8 22.1 %copy-start.11 = (bf16[96]{0:T(256)(128)(2,1)S(1)}, bf16[96]{0:T(256)(128)(2,1)}, u32[]{:S(2)}) copy-start(bf16[96]{0:T(256)(128)(2,1)} %param.22) | copy-start | bytes 580
  241.9 12.3 %collective-permute-start.24 = (f32[8,2048]{1,0:T(8,128)S(1)}, f32[8,2048]{1,0:T(8,128)S(1)}, u32[]{:S(2)}, u32[]{:S(2)}) collective-permute-start(f32[8,2048]{1,0:T(8,128)S(1)} %add.265), channel_id=1, source_target_pairs={{0,16},{2,18},{4,20},{6,22},{8,24},{10,26},{12,28},{14,30},{16,0},... | collective-permute-start | bytes 196616 | tf_op jit(solution)/shard_map/ppermute | solution.py:536
  242.7 19.3 %collective-permute-start.19 = (bf16[192,768]{1,0:T(8,128)(2,1)}, bf16[192,768]{1,0:T(8,128)(2,1)S(1)}, u32[]{:S(2)}, u32[]{:S(2)}) collective-permute-start(bf16[192,768]{1,0:T(8,128)(2,1)} %reduce-scatter.2.cloned.1.call-done), channel_id=1, source_target_pairs={{0,1},{1,0},{2,3},{3,2},{4,5},{5,4},{6,7},{7,6},{8,9},{9,8},{10,11... | collective-permute-start | bytes 884744 | tf_op jit(solution)/shard_map/ppermute | solution.py:536
  242.7 11.5 %collective-permute-start.18 = (f32[16,768]{1,0:T(8,128)S(1)}, f32[16,768]{1,0:T(8,128)S(1)}, u32[]{:S(2)}, u32[]{:S(2)}) collective-permute-start(f32[16,768]{1,0:T(8,128)S(1)} %copy-done.15), channel_id=1, source_target_pairs={{1,0},{3,2},{5,4},{7,6},{9,8},{11,10},{13,12},{15,14},{17,16},{19,... | collective-permute-start | bytes 147464 | tf_op jit(solution)/shard_map/ppermute | solution.py:866
  244.1 16.2 %collective-permute-start.20 = (bf16[48,1920]{1,0:T(8,128)(2,1)S(1)}, bf16[48,1920]{1,0:T(8,128)(2,1)S(1)}, u32[]{:S(2)}, u32[]{:S(2)}) collective-permute-start(bf16[48,1920]{1,0:T(8,128)(2,1)S(1)} %get-tuple-element.124), channel_id=1, source_target_pairs={{0,8},{2,10},{4,12},{6,14},{8,16},{10,18},{12,20},{14,22},{16,24},... | collective-permute-start | bytes 552968 | tf_op jit(solution)/shard_map/ppermute | solution.py:540
  244.6 15.7 %collective-permute-start.21 = (bf16[48,1920]{1,0:T(8,128)(2,1)S(1)}, bf16[48,1920]{1,0:T(8,128)(2,1)S(1)}, u32[]{:S(2)}, u32[]{:S(2)}) collective-permute-start(bf16[48,1920]{1,0:T(8,128)(2,1)S(1)} %get-tuple-element.126), channel_id=1, source_target_pairs={{0,16},{2,18},{4,20},{6,22},{8,24},{10,26},{12,28},{14,30},{16,0},... | collective-permute-start | bytes 552968 | tf_op jit(solution)/shard_map/ppermute | solution.py:540
  254.2 6.9 %collective-permute-start.22 = (bf16[48,1920]{1,0:T(8,128)(2,1)S(1)}, bf16[48,1920]{1,0:T(8,128)(2,1)S(1)}, u32[]{:S(2)}, u32[]{:S(2)}) collective-permute-start(bf16[48,1920]{1,0:T(8,128)(2,1)S(1)} %get-tuple-element.125), channel_id=1, source_target_pairs={{0,24},{2,26},{4,28},{6,30},{8,0},{10,2},{12,4},{14,6},{16,8},{18,... | collective-permute-start | bytes 552968 | tf_op jit(solution)/shard_map/ppermute | solution.py:540
  254.2 4.3 %collective-permute-start.25 = (f32[8,2048]{1,0:T(8,128)S(1)}, f32[8,2048]{1,0:T(8,128)S(1)}, u32[]{:S(2)}, u32[]{:S(2)}) collective-permute-start(f32[8,2048]{1,0:T(8,128)S(1)} %add.283), channel_id=1, source_target_pairs={{0,1},{1,0},{2,3},{3,2},{4,5},{5,4},{6,7},{7,6},{8,9},{9,8},{10,11... | collective-permute-start | bytes 196616 | tf_op jit(solution)/shard_map/ppermute | solution.py:536
  261.2 7.5 %copy-start.8 = (bf16[48]{0:T(256)(128)(2,1)S(1)}, bf16[48]{0:T(256)(128)(2,1)}, u32[]{:S(2)}) copy-start(bf16[48]{0:T(256)(128)(2,1)} %param.14) | copy-start | bytes 292
  261.2 5.6 %collective-permute-start.23 = (bf16[48,1920]{1,0:T(8,128)(2,1)S(1)}, bf16[48,1920]{1,0:T(8,128)(2,1)S(1)}, u32[]{:S(2)}, u32[]{:S(2)}) collective-permute-start(bf16[48,1920]{1,0:T(8,128)(2,1)S(1)} %fusion.13), channel_id=1, source_target_pairs={{0,1},{1,0},{2,3},{3,2},{4,5},{5,4},{6,7},{7,6},{8,9},{9,8},{10,11... | collective-permute-start | bytes 552968 | tf_op jit(solution)/shard_map/ppermute | solution.py:536
Sparse Core Ops, SparseCore 0:
  26.4 58.4 all-gather.1
  139.6 75.9 reduce-scatter.1
